TPU v7x, 128 devices: a whole 4x4x4 slice. The times are simulated.
128 devices in a mesh: lon: 64 (over y_lo, x, z, core), lat: 2 (over y_hi).
Axes of the slice: x: 4, y: 4 (y_hi: 2, y_lo: 2; y = y_hi * 2 + y_lo), z: 4, core: 2. Of those that a mesh axis runs over, the one named last changes fastest.
Arguments:
- tracers: float32 [3, 10, 128, 8192], P(None, None, 'lat', 'lon'), may hold values from -6 to 6
- offsets: int32 [10, 128, 8192], P(None, 'lat', 'lon'), may hold values from -16 to 15, as said below
- weights: float32 [10, 128, 8192], P(None, 'lat', 'lon'), may hold values from 0 to 1
- diffusion: float32 [9, 128, 8192], P(None, 'lat', 'lon'), may hold values from 0.05 to 5
- send_index: int32 [128, 128, 128], P(('lon', 'lat')), may hold values from 0 to 8191, as said below
- send_count: int32 [128, 128], P(('lon', 'lat')), may hold values from 1 to 128, as said below
Outputs:
- owned_tracers: float32 [3, 10, 1048576], P(None, None, ('lon', 'lat'))
Inputs may be any that keep to these rules, and one draw needn't show every extreme that they name: `offsets`: the departure interval of a cell starts this many cells east of it on the same row and level; both ends of the range occur. `send_count`: entry [d, e] counts the columns of device d that device e owns. Every row and every column sums to 8192. A device keeps exactly 127 of its own columns and sends exactly one to the device 128 // 2 further on; some list holds exactly 128 columns. `send_index`: entries [d, e, 0 : send_count[d, e]] are local column indices of device d that device e owns, in owner order; each column of d appears in exactly one list once; entries past the count are valid column indices that carry no meaning.
All inputs are finite; a program needn't handle non-finite values.
Results may differ from a plain program's by a relative error of at most 0.0003.
Values sent between devices are 32-bit elements; how exact they have to be, the bound alone decides.
A program may use at most 128 MiB of HBM per device.

v0:
```python
import jax
import jax.numpy as jnp
from jax import lax
from jax.sharding import PartitionSpec as P

NTR = 3
LEV = 10
HALO = 16


def shifted(block, axis, distance):
    devices = range(lax.axis_size(axis))
    route = [((i - distance) % len(devices), i) for i in devices]
    return lax.ppermute(block, axis, route)


def solve_columns(values, coef_rows):
    levels = values.shape[1]
    diag = []
    for level in range(levels):
        term = jnp.ones_like(coef_rows[0])
        if level > 0:
            term = term + coef_rows[level - 1]
        if level < levels - 1:
            term = term + coef_rows[level]
        diag.append(term)
    upper = []
    reduced = []
    denom = diag[0]
    upper.append(-coef_rows[0] / denom)
    reduced.append(values[:, 0] / denom)
    for level in range(1, levels):
        denom = diag[level] + coef_rows[level - 1] * upper[level - 1]
        reduced.append((values[:, level] + coef_rows[level - 1] * reduced[level - 1]) / denom)
        if level < levels - 1:
            upper.append(-coef_rows[level] / denom)
    output = [None] * levels
    output[levels - 1] = reduced[levels - 1]
    for level in range(levels - 2, -1, -1):
        output[level] = reduced[level] - upper[level] * output[level + 1]
    return jnp.stack(output, axis=1)


def pick_columns(source, index):
    total = index.shape[0]
    width = source.shape[1]
    block = 512
    blocks = index.reshape(total // block, block)
    column_ids = jnp.arange(width, dtype=jnp.int32)

    def one_block(block_index):
        selector = (column_ids[:, None] == block_index[None, :]).astype(jnp.float32)
        return jnp.dot(
            source, selector, precision=lax.Precision.HIGHEST, preferred_element_type=jnp.float32
        )

    picked = lax.map(one_block, blocks)
    return jnp.moveaxis(picked, 0, 1).reshape(source.shape[0], total)


def place_owned(arrived, counts_in, columns):
    peer_count = lax.axis_size(("lon", "lat"))
    own_index = lax.axis_index(("lon", "lat"))
    slot_width = arrived.shape[1] // peer_count
    by_source = counts_in[0].astype(jnp.int32)
    counts = jnp.roll(by_source[::-1], own_index + 1)
    seg_ends = jnp.cumsum(counts)
    places = jnp.arange(columns, dtype=jnp.int32)
    passed = seg_ends[:, None] <= places[None, :]
    segment = jnp.sum(passed.astype(jnp.int32), axis=0)
    seg_start = jnp.sum(jnp.where(passed, counts[:, None], 0), axis=0)
    source = (own_index - segment) % peer_count
    column = source * slot_width + places - seg_start
    return pick_columns(arrived, column)


def body(tracers, offsets, weights, diffusion, send_index, send_count):
    lon_width = tracers.shape[3]
    from_west = shifted(tracers[..., lon_width - HALO :], "lon", 1)
    from_east = shifted(tracers[..., :HALO], "lon", -1)
    extended = jnp.concatenate([from_west, tracers, from_east], axis=3)
    start_shift = offsets + HALO
    advected = jnp.zeros(tracers.shape, jnp.float32)
    for shift_value in range(2 * HALO + 1):
        west_part = jnp.where(start_shift == shift_value, 1.0 - weights, 0.0)
        east_part = jnp.where(start_shift + 1 == shift_value, weights, 0.0)
        window = extended[..., shift_value : shift_value + lon_width]
        advected = advected + west_part[None] * window
        advected = advected + east_part[None] * window
    columns = tracers.shape[2] * lon_width
    row_block = advected.reshape(NTR * LEV, columns)
    coef_rows = diffusion.reshape(LEV - 1, columns)
    index_flat = send_index[0].reshape(-1)
    counts_out = send_count.astype(jnp.float32)
    stacked = jnp.concatenate([row_block, coef_rows], axis=0)
    packed = pick_columns(stacked, index_flat)
    arrived, counts_in = (
        lax.all_to_all(packed, ("lon", "lat"), split_axis=1, concat_axis=1, tiled=True),
        lax.all_to_all(counts_out, ("lon", "lat"), split_axis=1, concat_axis=1, tiled=True),
    )
    owned = place_owned(arrived, counts_in, columns)
    values = owned[: NTR * LEV].reshape(NTR, LEV, columns)
    result = solve_columns(values, owned[NTR * LEV :])
    return result


def solution(mesh):
    return jax.shard_map(
        body,
        mesh=mesh,
        in_specs=(
            P(None, None, "lat", "lon"),
            P(None, "lat", "lon"),
            P(None, "lat", "lon"),
            P(None, "lat", "lon"),
            P(("lon", "lat"), None, None),
            P(("lon", "lat"), None),
        ),
        out_specs=P(None, None, ("lon", "lat")),
        check_vma=False,
    )
```

profile of v0, /device:TPU:1, one launch (start us, length us, event | category | flops | bytes accessed | tf_op | source)
XLA Modules:
  0.0 539.5 jit_solution(11046402633426692024)
XLA Ops:
  6.4 10.2 %all-to-all-start = ((f32[1,128,1]{2,0,1:T(1,128)}), f32[1,128,1]{2,0,1:T(1,128)S(1)}, u32[]{:S(2)}, u32[]{:S(2)}) async-start(f32[1,128,1]{2,0,1:T(1,128)} %copy.33), calls=%async_computation | async-start | bytes 131072 | tf_op jit(solution)/shard_map/all_to_all | solution.py:99
  16.7 8.5 %compare_select_fusion.63 = (f32[10,64,128]{2,1,0:T(8,128)}, f32[10,64,128]{2,1,0:T(8,128)}, f32[10,64,128]{2,1,0:T(8,128)}, f32[10,64,128]{2,1,0:T(8,128)}, f32...) fusion(f32[10,64,128]{2,1,0:T(8,128)S(1)} %copy-done.1, ...), kind=kLoop, calls=%fused_computation.197 | loop fusion | flops 11141120 | bytes 21954560 | tf_op jit(solution)/shard_map/jit(_where)/select_n | solution.py:85
  27.8 22.4 %multiply_add_fusion = f32[3,10,64,128]{3,2,1,0:T(8,128)S(1)} fusion(f32[3,10,64,16]{3,2,1,0:T(8,128)S(1)} %copy.38, f32[3,10,64,128]{3,2,1,0:T(8,128)S(1)} %copy-done, f32[3,10,64,16]{3,2,1,0:T(8,128)S(1)} %copy.36, f32[10,64,128]{2,1,0:T(8,128)} %get-tuple-element.205, f32[10,64,128]{2,1,0:T(8,128)} %get-tuple-element.206, ...), kind=kLoop, calls=%fused_computation.132 | loop fusion | flops 39567360 | bytes 23511040 | tf_op jit(solution)/shard_map/add | solution.py:89
  51.1 225.1 %while.22 = (s32[]{:T(128)}, f32[32,39,512]{2,1,0:T(8,128)}, s32[32,512]{1,0:T(8,128)}, f32[39,8192]{1,0:T(8,128)S(1)}, s32[]{:T(128)}) while((s32[]{:T(128)}, f32[32,39,512]{2,1,0:T(8,128)}, s32[32,512]{1,0:T(8,128)}, f32[39,8192]{1,0:T(8,128)S(1)}, s32[]{:T(128)}) %tuple.139), condition=%wide.region_4.5_spmd.clone, body=%wide.region_3.4_spmd.clone.sunk | while | flops 1967128576 | bytes 1366593 | solution.py:57
  58.8 6.3 %fusion.94 = f32[32,39,512]{2,1,0:T(8,128)} fusion(f32[32,39,512]{2,1,0:T(8,128)} %get-tuple-element.268, s32[]{:T(128)} %get-tuple-element.267, f32[39,8192]{1,0:T(8,128)S(1)} %get-tuple-element.275, s32[512]{0:T(512)S(1)} %bitcast.88), kind=kOutput, calls=%fused_computation.6.clone.1 | convolution fusion | flops 1967128576 | bytes 1362432 | tf_op jit(solution)/shard_map/while/body/eval_jaxpr/dot_general | solution.py:53
  79.9 6.3 %fusion.94 = f32[32,39,512]{2,1,0:T(8,128)} fusion(f32[32,39,512]{2,1,0:T(8,128)} %get-tuple-element.268, s32[]{:T(128)} %get-tuple-element.267, f32[39,8192]{1,0:T(8,128)S(1)} %get-tuple-element.275, s32[512]{0:T(512)S(1)} %bitcast.88), kind=kOutput, calls=%fused_computation.6.clone.1 | convolution fusion | flops 1967128576 | bytes 1362432 | tf_op jit(solution)/shard_map/while/body/eval_jaxpr/dot_general | solution.py:53
  101.0 6.3 %fusion.94 = f32[32,39,512]{2,1,0:T(8,128)} fusion(f32[32,39,512]{2,1,0:T(8,128)} %get-tuple-element.268, s32[]{:T(128)} %get-tuple-element.267, f32[39,8192]{1,0:T(8,128)S(1)} %get-tuple-element.275, s32[512]{0:T(512)S(1)} %bitcast.88), kind=kOutput, calls=%fused_computation.6.clone.1 | convolution fusion | flops 1967128576 | bytes 1362432 | tf_op jit(solution)/shard_map/while/body/eval_jaxpr/dot_general | solution.py:53
  115.1 6.3 %fusion.94 = f32[32,39,512]{2,1,0:T(8,128)} fusion(f32[32,39,512]{2,1,0:T(8,128)} %get-tuple-element.268, s32[]{:T(128)} %get-tuple-element.267, f32[39,8192]{1,0:T(8,128)S(1)} %get-tuple-element.275, s32[512]{0:T(512)S(1)} %bitcast.88), kind=kOutput, calls=%fused_computation.6.clone.1 | convolution fusion | flops 1967128576 | bytes 1362432 | tf_op jit(solution)/shard_map/while/body/eval_jaxpr/dot_general | solution.py:53
  157.3 6.3 %fusion.94 = f32[32,39,512]{2,1,0:T(8,128)} fusion(f32[32,39,512]{2,1,0:T(8,128)} %get-tuple-element.268, s32[]{:T(128)} %get-tuple-element.267, f32[39,8192]{1,0:T(8,128)S(1)} %get-tuple-element.275, s32[512]{0:T(512)S(1)} %bitcast.88), kind=kOutput, calls=%fused_computation.6.clone.1 | convolution fusion | flops 1967128576 | bytes 1362432 | tf_op jit(solution)/shard_map/while/body/eval_jaxpr/dot_general | solution.py:53
  199.5 6.3 %fusion.94 = f32[32,39,512]{2,1,0:T(8,128)} fusion(f32[32,39,512]{2,1,0:T(8,128)} %get-tuple-element.268, s32[]{:T(128)} %get-tuple-element.267, f32[39,8192]{1,0:T(8,128)S(1)} %get-tuple-element.275, s32[512]{0:T(512)S(1)} %bitcast.88), kind=kOutput, calls=%fused_computation.6.clone.1 | convolution fusion | flops 1967128576 | bytes 1362432 | tf_op jit(solution)/shard_map/while/body/eval_jaxpr/dot_general | solution.py:53
  206.6 6.3 %fusion.94 = f32[32,39,512]{2,1,0:T(8,128)} fusion(f32[32,39,512]{2,1,0:T(8,128)} %get-tuple-element.268, s32[]{:T(128)} %get-tuple-element.267, f32[39,8192]{1,0:T(8,128)S(1)} %get-tuple-element.275, s32[512]{0:T(512)S(1)} %bitcast.88), kind=kOutput, calls=%fused_computation.6.clone.1 | convolution fusion | flops 1967128576 | bytes 1362432 | tf_op jit(solution)/shard_map/while/body/eval_jaxpr/dot_general | solution.py:53
  213.6 6.3 %fusion.94 = f32[32,39,512]{2,1,0:T(8,128)} fusion(f32[32,39,512]{2,1,0:T(8,128)} %get-tuple-element.268, s32[]{:T(128)} %get-tuple-element.267, f32[39,8192]{1,0:T(8,128)S(1)} %get-tuple-element.275, s32[512]{0:T(512)S(1)} %bitcast.88), kind=kOutput, calls=%fused_computation.6.clone.1 | convolution fusion | flops 1967128576 | bytes 1362432 | tf_op jit(solution)/shard_map/while/body/eval_jaxpr/dot_general | solution.py:53
  241.8 6.3 %fusion.94 = f32[32,39,512]{2,1,0:T(8,128)} fusion(f32[32,39,512]{2,1,0:T(8,128)} %get-tuple-element.268, s32[]{:T(128)} %get-tuple-element.267, f32[39,8192]{1,0:T(8,128)S(1)} %get-tuple-element.275, s32[512]{0:T(512)S(1)} %bitcast.88), kind=kOutput, calls=%fused_computation.6.clone.1 | convolution fusion | flops 1967128576 | bytes 1362432 | tf_op jit(solution)/shard_map/while/body/eval_jaxpr/dot_general | solution.py:53
  285.7 9.8 %all-to-all-start.1 = ((f32[39,128,128]{2,0,1:T(8,128)}), f32[39,128,128]{2,0,1:T(8,128)S(1)}, u32[]{:S(2)}, u32[]{:S(2)}) async-start(f32[39,128,128]{2,0,1:T(8,128)} %copy.40), calls=%async_computation.1 | async-start | bytes 5242880 | tf_op jit(solution)/shard_map/all_to_all | solution.py:98
  299.7 31.0 %all-to-all-done.1 = f32[39,128,128]{2,0,1:T(8,128)S(1)} async-done(((f32[39,128,128]{2,0,1:T(8,128)}), f32[39,128,128]{2,0,1:T(8,128)S(1)}, u32[]{:S(2)}, u32[]{:S(2)}) %all-to-all-start.1) | async-done | bytes 2555936 | tf_op jit(solution)/shard_map/all_to_all | solution.py:98
  332.9 190.5 %while.23 = (s32[]{:T(128)}, f32[16,39,512]{2,1,0:T(8,128)}, s32[16,512]{1,0:T(8,128)S(1)}, f32[39,16384]{1,0:T(8,128)S(1)}, s32[]{:T(128)}) while((s32[]{:T(128)}, f32[16,39,512]{2,1,0:T(8,128)}, s32[16,512]{1,0:T(8,128)S(1)}, f32[39,16384]{1,0:T(8,128)S(1)}, s32[]{:T(128)}) %tuple.145), condition=%wide.region_6.7_spmd.clone, body=%wide.region_5.6_spmd.clone.sunk | while | flops 3934257152 | bytes 2644545 | solution.py:57
  333.2 11.9 %fusion.96 = f32[16,39,512]{2,1,0:T(8,128)} fusion(f32[16,39,512]{2,1,0:T(8,128)} %get-tuple-element.283, s32[]{:T(128)} %get-tuple-element.282, f32[39,16384]{1,0:T(8,128)S(1)} %get-tuple-element.290, s32[512]{0:T(512)S(1)} %bitcast.89), kind=kOutput, calls=%fused_computation.12.clone.1 | convolution fusion | flops 3934257152 | bytes 2640384 | tf_op jit(solution)/shard_map/while/body/eval_jaxpr/dot_general | solution.py:53
  345.1 11.9 %fusion.96 = f32[16,39,512]{2,1,0:T(8,128)} fusion(f32[16,39,512]{2,1,0:T(8,128)} %get-tuple-element.283, s32[]{:T(128)} %get-tuple-element.282, f32[39,16384]{1,0:T(8,128)S(1)} %get-tuple-element.290, s32[512]{0:T(512)S(1)} %bitcast.89), kind=kOutput, calls=%fused_computation.12.clone.1 | convolution fusion | flops 3934257152 | bytes 2640384 | tf_op jit(solution)/shard_map/while/body/eval_jaxpr/dot_general | solution.py:53
  357.0 11.9 %fusion.96 = f32[16,39,512]{2,1,0:T(8,128)} fusion(f32[16,39,512]{2,1,0:T(8,128)} %get-tuple-element.283, s32[]{:T(128)} %get-tuple-element.282, f32[39,16384]{1,0:T(8,128)S(1)} %get-tuple-element.290, s32[512]{0:T(512)S(1)} %bitcast.89), kind=kOutput, calls=%fused_computation.12.clone.1 | convolution fusion | flops 3934257152 | bytes 2640384 | tf_op jit(solution)/shard_map/while/body/eval_jaxpr/dot_general | solution.py:53
  368.9 11.9 %fusion.96 = f32[16,39,512]{2,1,0:T(8,128)} fusion(f32[16,39,512]{2,1,0:T(8,128)} %get-tuple-element.283, s32[]{:T(128)} %get-tuple-element.282, f32[39,16384]{1,0:T(8,128)S(1)} %get-tuple-element.290, s32[512]{0:T(512)S(1)} %bitcast.89), kind=kOutput, calls=%fused_computation.12.clone.1 | convolution fusion | flops 3934257152 | bytes 2640384 | tf_op jit(solution)/shard_map/while/body/eval_jaxpr/dot_general | solution.py:53
  380.8 11.9 %fusion.96 = f32[16,39,512]{2,1,0:T(8,128)} fusion(f32[16,39,512]{2,1,0:T(8,128)} %get-tuple-element.283, s32[]{:T(128)} %get-tuple-element.282, f32[39,16384]{1,0:T(8,128)S(1)} %get-tuple-element.290, s32[512]{0:T(512)S(1)} %bitcast.89), kind=kOutput, calls=%fused_computation.12.clone.1 | convolution fusion | flops 3934257152 | bytes 2640384 | tf_op jit(solution)/shard_map/while/body/eval_jaxpr/dot_general | solution.py:53
  392.6 11.9 %fusion.96 = f32[16,39,512]{2,1,0:T(8,128)} fusion(f32[16,39,512]{2,1,0:T(8,128)} %get-tuple-element.283, s32[]{:T(128)} %get-tuple-element.282, f32[39,16384]{1,0:T(8,128)S(1)} %get-tuple-element.290, s32[512]{0:T(512)S(1)} %bitcast.89), kind=kOutput, calls=%fused_computation.12.clone.1 | convolution fusion | flops 3934257152 | bytes 2640384 | tf_op jit(solution)/shard_map/while/body/eval_jaxpr/dot_general | solution.py:53
  404.5 11.9 %fusion.96 = f32[16,39,512]{2,1,0:T(8,128)} fusion(f32[16,39,512]{2,1,0:T(8,128)} %get-tuple-element.283, s32[]{:T(128)} %get-tuple-element.282, f32[39,16384]{1,0:T(8,128)S(1)} %get-tuple-element.290, s32[512]{0:T(512)S(1)} %bitcast.89), kind=kOutput, calls=%fused_computation.12.clone.1 | convolution fusion | flops 3934257152 | bytes 2640384 | tf_op jit(solution)/shard_map/while/body/eval_jaxpr/dot_general | solution.py:53
  416.4 11.9 %fusion.96 = f32[16,39,512]{2,1,0:T(8,128)} fusion(f32[16,39,512]{2,1,0:T(8,128)} %get-tuple-element.283, s32[]{:T(128)} %get-tuple-element.282, f32[39,16384]{1,0:T(8,128)S(1)} %get-tuple-element.290, s32[512]{0:T(512)S(1)} %bitcast.89), kind=kOutput, calls=%fused_computation.12.clone.1 | convolution fusion | flops 3934257152 | bytes 2640384 | tf_op jit(solution)/shard_map/while/body/eval_jaxpr/dot_general | solution.py:53
  428.3 11.9 %fusion.96 = f32[16,39,512]{2,1,0:T(8,128)} fusion(f32[16,39,512]{2,1,0:T(8,128)} %get-tuple-element.283, s32[]{:T(128)} %get-tuple-element.282, f32[39,16384]{1,0:T(8,128)S(1)} %get-tuple-element.290, s32[512]{0:T(512)S(1)} %bitcast.89), kind=kOutput, calls=%fused_computation.12.clone.1 | convolution fusion | flops 3934257152 | bytes 2640384 | tf_op jit(solution)/shard_map/while/body/eval_jaxpr/dot_general | solution.py:53
  440.2 11.9 %fusion.96 = f32[16,39,512]{2,1,0:T(8,128)} fusion(f32[16,39,512]{2,1,0:T(8,128)} %get-tuple-element.283, s32[]{:T(128)} %get-tuple-element.282, f32[39,16384]{1,0:T(8,128)S(1)} %get-tuple-element.290, s32[512]{0:T(512)S(1)} %bitcast.89), kind=kOutput, calls=%fused_computation.12.clone.1 | convolution fusion | flops 3934257152 | bytes 2640384 | tf_op jit(solution)/shard_map/while/body/eval_jaxpr/dot_general | solution.py:53
  452.1 11.9 %fusion.96 = f32[16,39,512]{2,1,0:T(8,128)} fusion(f32[16,39,512]{2,1,0:T(8,128)} %get-tuple-element.283, s32[]{:T(128)} %get-tuple-element.282, f32[39,16384]{1,0:T(8,128)S(1)} %get-tuple-element.290, s32[512]{0:T(512)S(1)} %bitcast.89), kind=kOutput, calls=%fused_computation.12.clone.1 | convolution fusion | flops 3934257152 | bytes 2640384 | tf_op jit(solution)/shard_map/while/body/eval_jaxpr/dot_general | solution.py:53
  464.0 11.9 %fusion.96 = f32[16,39,512]{2,1,0:T(8,128)} fusion(f32[16,39,512]{2,1,0:T(8,128)} %get-tuple-element.283, s32[]{:T(128)} %get-tuple-element.282, f32[39,16384]{1,0:T(8,128)S(1)} %get-tuple-element.290, s32[512]{0:T(512)S(1)} %bitcast.89), kind=kOutput, calls=%fused_computation.12.clone.1 | convolution fusion | flops 3934257152 | bytes 2640384 | tf_op jit(solution)/shard_map/while/body/eval_jaxpr/dot_general | solution.py:53
  475.9 11.9 %fusion.96 = f32[16,39,512]{2,1,0:T(8,128)} fusion(f32[16,39,512]{2,1,0:T(8,128)} %get-tuple-element.283, s32[]{:T(128)} %get-tuple-element.282, f32[39,16384]{1,0:T(8,128)S(1)} %get-tuple-element.290, s32[512]{0:T(512)S(1)} %bitcast.89), kind=kOutput, calls=%fused_computation.12.clone.1 | convolution fusion | flops 3934257152 | bytes 2640384 | tf_op jit(solution)/shard_map/while/body/eval_jaxpr/dot_general | solution.py:53
  487.8 11.9 %fusion.96 = f32[16,39,512]{2,1,0:T(8,128)} fusion(f32[16,39,512]{2,1,0:T(8,128)} %get-tuple-element.283, s32[]{:T(128)} %get-tuple-element.282, f32[39,16384]{1,0:T(8,128)S(1)} %get-tuple-element.290, s32[512]{0:T(512)S(1)} %bitcast.89), kind=kOutput, calls=%fused_computation.12.clone.1 | convolution fusion | flops 3934257152 | bytes 2640384 | tf_op jit(solution)/shard_map/while/body/eval_jaxpr/dot_general | solution.py:53
  499.7 11.9 %fusion.96 = f32[16,39,512]{2,1,0:T(8,128)} fusion(f32[16,39,512]{2,1,0:T(8,128)} %get-tuple-element.283, s32[]{:T(128)} %get-tuple-element.282, f32[39,16384]{1,0:T(8,128)S(1)} %get-tuple-element.290, s32[512]{0:T(512)S(1)} %bitcast.89), kind=kOutput, calls=%fused_computation.12.clone.1 | convolution fusion | flops 3934257152 | bytes 2640384 | tf_op jit(solution)/shard_map/while/body/eval_jaxpr/dot_general | solution.py:53
  511.6 11.9 %fusion.96 = f32[16,39,512]{2,1,0:T(8,128)} fusion(f32[16,39,512]{2,1,0:T(8,128)} %get-tuple-element.283, s32[]{:T(128)} %get-tuple-element.282, f32[39,16384]{1,0:T(8,128)S(1)} %get-tuple-element.290, s32[512]{0:T(512)S(1)} %bitcast.89), kind=kOutput, calls=%fused_computation.12.clone.1 | convolution fusion | flops 3934257152 | bytes 2640384 | tf_op jit(solution)/shard_map/while/body/eval_jaxpr/dot_general | solution.py:53
  (138 shorter events, 210.1 us)
Async XLA Ops:
  0.0 5.7 %copy-start.5 = (s32[1,128]{1,0:T(1,128)S(1)}, s32[1,128]{1,0:T(1,128)}, u32[]{:S(2)}) copy-start(s32[1,128]{1,0:T(1,128)} %param.15) | copy-start | bytes 1540
  0.0 16.6 %copy-start.2 = (s32[10,64,128]{2,1,0:T(8,128)S(1)}, s32[10,64,128]{2,1,0:T(8,128)}, u32[]{:S(2)}) copy-start(s32[10,64,128]{2,1,0:T(8,128)} %param.11) | copy-start | bytes 983044
  0.0 16.6 %copy-start.1 = (f32[10,64,128]{2,1,0:T(8,128)S(1)}, f32[10,64,128]{2,1,0:T(8,128)}, u32[]{:S(2)}) copy-start(f32[10,64,128]{2,1,0:T(8,128)} %param.12) | copy-start | bytes 983044
  2.2 23.9 %collective-permute-start = (f32[3,10,64,16]{2,3,1,0:T(8,128)S(1)}, f32[3,10,64,16]{2,3,1,0:T(8,128)S(1)}, u32[]{:S(2)}, u32[]{:S(2)}) collective-permute-start(f32[3,10,64,16]{2,3,1,0:T(8,128)S(1)} %copy.44), channel_id=1, source_target_pairs={{126,0},{0,2},{2,4},{4,6},{6,8},{8,10},{10,12},{12,14},{14,16},{16... | collective-permute-start | bytes 368648 | tf_op jit(solution)/shard_map/ppermute | solution.py:14
  5.6 20.9 %collective-permute-start.1 = (f32[3,10,64,16]{2,3,1,0:T(8,128)S(1)}, f32[3,10,64,16]{2,3,1,0:T(8,128)}, u32[]{:S(2)}, u32[]{:S(2)}) collective-permute-start(f32[3,10,64,16]{2,3,1,0:T(8,128)S(1)} %copy.45), channel_id=1, source_target_pairs={{2,0},{4,2},{6,4},{8,6},{10,8},{12,10},{14,12},{16,14},{18,16},{20... | collective-permute-start | bytes 368648 | tf_op jit(solution)/shard_map/ppermute | solution.py:14
  6.4 279.3 %all-to-all-start = ((f32[1,128,1]{2,0,1:T(1,128)}), f32[1,128,1]{2,0,1:T(1,128)S(1)}, u32[]{:S(2)}, u32[]{:S(2)}) async-start(f32[1,128,1]{2,0,1:T(1,128)} %copy.33), calls=%async_computation | async-start | bytes 131072 | tf_op jit(solution)/shard_map/all_to_all | solution.py:99
  16.6 8.5 %copy-start.3 = (f32[9,64,128]{2,1,0:T(8,128)S(1)}, f32[9,64,128]{2,1,0:T(8,128)}, u32[]{:S(2)}) copy-start(f32[9,64,128]{2,1,0:T(8,128)} %param.13) | copy-start | bytes 884740
  16.6 8.9 %copy-start.4 = (s32[1,128,128]{2,1,0:T(8,128)S(1)}, s32[1,128,128]{2,1,0:T(8,128)}, u32[]{:S(2)}) copy-start(s32[1,128,128]{2,1,0:T(8,128)} %param.14) | copy-start | bytes 196612
  25.1 2.7 copy-start
  285.7 44.9 %all-to-all-start.1 = ((f32[39,128,128]{2,0,1:T(8,128)}), f32[39,128,128]{2,0,1:T(8,128)S(1)}, u32[]{:S(2)}, u32[]{:S(2)}) async-start(f32[39,128,128]{2,0,1:T(8,128)} %copy.40), calls=%async_computation.1 | async-start | bytes 5242880 | tf_op jit(solution)/shard_map/all_to_all | solution.py:98
where the time goes:
time: 543 us; the launch traced here: 539 us
  matrix products  392 us (72%)
  local copies, waits for them, and re-layouts  49.9 us (9%)
  other arithmetic  42.7 us (8%)
  waiting for transfers between devices  31 us (6%)
  starting transfers between devices  23.1 us (4%)
    dot_general x48, matrix products, one_block(): jnp.dot(source, selector, precision=lax.Precision.HIGHEST, preferred_elem...  392 us
    all_to_all x1, waiting for transfers between devices, body(): lax.all_to_all(packed, ('lon', 'lat'), split_axis=1, concat_axis=1, tiled...  31 us
    dynamic_slice x48, local copies, waits for them, and re-layouts, pick_columns(): picked = lax.map(one_block, blocks)  23.2 us
    add x1, other arithmetic, body(): advected = advected + east_part[None] * window  22.4 us
  transfers between devices with their start and end apart: 4, of which 1 were waited for; matrix products, arithmetic and copies ran while one was open for 50% of the time, Pallas kernels for 0%

commit v1 on v0

v1 whole, which is shorter than its diff:
```python
import jax
import jax.numpy as jnp
from jax import lax
from jax.experimental import pallas as pl
from jax.experimental.pallas import tpu as pltpu
from jax.sharding import PartitionSpec as P

NTR = 3
LEV = 10
HALO = 16
FEAT = 32
LANES = 128
AXES = ("lon", "lat")


def shifted(block, axis, distance):
    devices = range(lax.axis_size(axis))
    route = [((i - distance) % len(devices), i) for i in devices]
    return lax.ppermute(block, axis, route)


def solve_levels(values, coefs):
    upper, reduced = [], [[] for _ in values]
    for level in range(LEV):
        denom = jnp.ones_like(coefs[0])
        if level > 0:
            denom = denom + coefs[level - 1]
        if level < LEV - 1:
            denom = denom + coefs[level]
        if level > 0:
            denom = denom - coefs[level - 1] * upper[level - 1]
        inverse = 1.0 / denom
        if level < LEV - 1:
            upper.append(coefs[level] * inverse)
        for t in range(len(values)):
            right = values[t][level]
            if level > 0:
                right = right + coefs[level - 1] * reduced[t][level - 1]
            reduced[t].append(right * inverse)
    output = [[None] * LEV for _ in values]
    for t in range(len(values)):
        output[t][LEV - 1] = reduced[t][LEV - 1]
        for level in range(LEV - 2, -1, -1):
            output[t][level] = reduced[t][level] + upper[level] * output[t][level + 1]
    return output


def pack_kernel(tracers, halo, offsets, weights, diffusion, index, count, packed, rows, table, stage):
    lat_rows = tracers.shape[2]
    peers = packed.shape[0]
    lane = lax.broadcasted_iota(jnp.int32, (8, LANES), 1)

    def advect_group(group, carry):
        at = pl.ds(pl.multiple_of(group * 8, 8), 8)
        values = [[] for _ in range(NTR)]
        for level in range(LEV):
            cell = lane + offsets[level, at, :]
            weight = weights[level, at, :]
            west_in = (cell >= 0) & (cell < LANES)
            west_at = cell & (LANES - 1)
            east_in = (cell >= -1) & (cell < LANES - 1)
            east_at = (cell + 1) & (LANES - 1)
            for t in range(NTR):
                main = tracers[t, level, at, :]
                edge = halo[t, level, at, :]
                west = jnp.where(
                    west_in,
                    jnp.take_along_axis(main, west_at, axis=1),
                    jnp.take_along_axis(edge, west_at, axis=1),
                )
                east = jnp.where(
                    east_in,
                    jnp.take_along_axis(main, east_at, axis=1),
                    jnp.take_along_axis(edge, east_at, axis=1),
                )
                values[t].append((1.0 - weight) * west + weight * east)
        coefs = [diffusion[level, at, :] for level in range(LEV - 1)]
        solved = solve_levels(values, coefs)
        for t in range(NTR):
            for level in range(LEV):
                rows[pl.ds(group * 8 * FEAT + t * LEV + level, 8, stride=FEAT), :] = solved[t][level]
        for spare in range(NTR * LEV, FEAT):
            rows[pl.ds(group * 8 * FEAT + spare, 8, stride=FEAT), :] = jnp.zeros((8, LANES), jnp.float32)
        return carry

    lax.fori_loop(0, lat_rows // 8, advect_group, 0)

    def turn(row, carry):
        block = rows[pl.ds(pl.multiple_of(row * FEAT, FEAT), FEAT), :]
        wide = jnp.concatenate([block] * (LANES // FEAT), axis=0)
        table[pl.ds(pl.multiple_of(row * LANES, LANES), LANES), :] = wide.T
        return carry

    lax.fori_loop(0, lat_rows, turn, 0)

    four = LANES // FEAT
    lane_group = lax.broadcasted_iota(jnp.int32, (LANES, LANES), 1) // FEAT

    def pick(step, carry):
        for slot in range(LANES):
            for member in range(four):
                column = index[step * four + member, slot]
                stage[member, slot : slot + 1, :] = table[pl.ds(column, 1), :]
        wide = stage[0]
        for member in range(1, four):
            wide = jnp.where(lane_group == member, stage[member], wide)
        turned = wide.T
        for member in range(four):
            packed[step * four + member] = turned[member * FEAT : (member + 1) * FEAT, :]
            length = count[0, step * four + member].astype(jnp.float32)
            packed[step * four + member, NTR * LEV : NTR * LEV + 1, :] = jnp.full((1, LANES), length, jnp.float32)
        return carry

    lax.fori_loop(0, peers // four, pick, 0)


def place_kernel(arrived, counts, out, owned):
    peers = arrived.shape[0]
    columns = out.shape[2]
    me = lax.axis_index(AXES)
    lane = lax.broadcasted_iota(jnp.int32, (FEAT, LANES), 1)

    def place(step, start):
        source = lax.rem(me - step + peers, peers)
        block = start // LANES
        shift = lax.rem(start, LANES)
        rolled = pltpu.roll(arrived[source], shift, 1)
        first = pl.ds(pl.multiple_of(block * FEAT, FEAT), FEAT)
        second = pl.ds(pl.multiple_of(block * FEAT + FEAT, FEAT), FEAT)
        owned[first, :] = jnp.where(lane >= shift, rolled, owned[first, :])
        owned[second, :] = rolled
        return start + counts[source]

    lax.fori_loop(0, peers, place, jnp.int32(0))

    for block in range(columns // LANES):
        for t in range(NTR):
            begin = block * FEAT + t * LEV
            out[t, :, block * LANES : (block + 1) * LANES] = owned[begin : begin + LEV, :]


def body(tracers, offsets, weights, diffusion, send_index, send_count):
    lat_rows, lon_width = tracers.shape[2:]
    peers = lax.axis_size(AXES)
    columns = lat_rows * lon_width
    from_west = shifted(tracers[..., lon_width - HALO :], "lon", 1)
    from_east = shifted(tracers[..., :HALO], "lon", -1)
    middle = jnp.zeros((*tracers.shape[:3], lon_width - 2 * HALO), jnp.float32)
    halo = jnp.concatenate([from_east, middle, from_west], axis=3)
    vmem = pl.BlockSpec(memory_space=pltpu.VMEM)
    smem = pl.BlockSpec(memory_space=pltpu.SMEM)
    packed = pl.pallas_call(
        pack_kernel,
        out_shape=jax.ShapeDtypeStruct((peers, FEAT, LANES), jnp.float32),
        in_specs=[vmem] * 5 + [smem] * 2,
        out_specs=vmem,
        scratch_shapes=[
            pltpu.VMEM((lat_rows * FEAT, LANES), jnp.float32),
            pltpu.VMEM((columns, LANES), jnp.float32),
            pltpu.VMEM((LANES // FEAT, LANES, LANES), jnp.float32),
        ],
        compiler_params=pltpu.CompilerParams(vmem_limit_bytes=40 << 20),
        name="advect_solve_pack",
    )(tracers, halo, offsets, weights, diffusion, send_index[0], send_count)
    arrived = lax.all_to_all(packed, AXES, split_axis=0, concat_axis=0, tiled=True)
    counts = arrived[:, NTR * LEV, 0].astype(jnp.int32)
    return pl.pallas_call(
        place_kernel,
        out_shape=jax.ShapeDtypeStruct((NTR, LEV, columns), jnp.float32),
        in_specs=[vmem, smem],
        out_specs=vmem,
        scratch_shapes=[pltpu.VMEM(((columns // LANES + 2) * FEAT, LANES), jnp.float32)],
        compiler_params=pltpu.CompilerParams(vmem_limit_bytes=32 << 20),
        name="place_owned",
    )(arrived, counts)


def solution(mesh):
    return jax.shard_map(
        body,
        mesh=mesh,
        in_specs=(
            P(None, None, "lat", "lon"),
            P(None, "lat", "lon"),
            P(None, "lat", "lon"),
            P(None, "lat", "lon"),
            P(("lon", "lat"), None, None),
            P(("lon", "lat"), None),
        ),
        out_specs=P(None, None, ("lon", "lat")),
        check_vma=False,
    )
```

time: 543 us -> 97.8 us (0.18)
  matrix products: 392 us -> 0 us
  local copies, waits for them, and re-layouts: 49.9 us -> 6.01 us
  blocking collectives: 0 us -> 42.1 us
  other arithmetic: 42.7 us -> 3.88 us
  Pallas kernels: 0 us -> 36.8 us
  waiting for transfers between devices: 31 us -> 5.67 us
  starting transfers between devices: 23.1 us -> 3.14 us
    dot_general x48 -> x0, matrix products: 392 us -> none  [one_block(): jnp.dot(source, selector, precision=lax.Precision.HIGHEST, preferred_elem...]
    all_to_all x0 -> x1, blocking collectives: none -> 42.1 us  [body(): lax.all_to_all(packed, AXES, split_axis=0, concat_axis=0, tiled=True)]
    pallas_call x0 -> x2, Pallas kernels: none -> 36.8 us  [the longest x1 26.9 us: body(): pl.pallas_call(pack_kernel, out_shape=jax.ShapeDtypeStruct((peers, FEAT,...]
    all_to_all x2 -> x0, waiting for transfers between devices: 31 us -> none  [the longest x1 31 us: body(): lax.all_to_all(packed, ('lon', 'lat'), split_axis=1, concat_axis=1, tiled...]
    dynamic_slice x49 -> x0, local copies, waits for them, and re-layouts: 23.3 us -> none  [the longest x48 23.2 us: pick_columns(): picked = lax.map(one_block, blocks)]
    add x2 -> x0, other arithmetic: 23 us -> none  [the longest x1 22.4 us: body(): advected = advected + east_part[None] * window]
    all_to_all x2 -> x0, starting transfers between devices: 20 us -> none  [the longest x1 10.2 us: body(): lax.all_to_all(counts_out, ('lon', 'lat'), split_axis=1, concat_axis=1, t...]
    select_n x1 -> x0, other arithmetic: 8.48 us -> none  [body(): west_part = jnp.where(start_shift == shift_value, 1.0 - weights, 0.0)]
  transfers between devices with their start and end apart: 4 -> 2, of which waited for: 1 -> 2; matrix products, arithmetic and copies ran while one was open for 50% -> 1% of each run, Pallas kernels for 0% -> 0%
where the time goes in v1:
time: 97.8 us; the launch traced here: 97.7 us
  blocking collectives  42.1 us (43%)
  Pallas kernels  36.8 us (38%)
  local copies, waits for them, and re-layouts  6.01 us (6%)
  waiting for transfers between devices  5.67 us (6%)
  other arithmetic  3.88 us (4%)
  starting transfers between devices  3.14 us (3%)
    all_to_all x1, blocking collectives, body(): lax.all_to_all(packed, AXES, split_axis=0, concat_axis=0, tiled=True)  42.1 us
    pallas_call x1, Pallas kernels, body(): pl.pallas_call(pack_kernel, out_shape=jax.ShapeDtypeStruct((peers, FEAT,...  26.9 us
    pallas_call x1, Pallas kernels, body(): pl.pallas_call(place_kernel, out_shape=jax.ShapeDtypeStruct((NTR, LEV, co...  9.82 us
    ppermute x2, waiting for transfers between devices, shifted(): return lax.ppermute(block, axis, route)  5.67 us
    ppermute x2, starting transfers between devices, shifted(): return lax.ppermute(block, axis, route)  3.14 us
    convert_element_type x1, other arithmetic, body(): counts = arrived[:, NTR * LEV, 0].astype(jnp.int32)  2.36 us
  transfers between devices with their start and end apart: 2, of which 2 were waited for; matrix products, arithmetic and copies ran while one was open for 1% of the time, Pallas kernels for 0%

profile of v1, /device:TPU:1, one launch (start us, length us, event | category | flops | bytes accessed | tf_op | source)
XLA Modules:
  0.0 97.7 jit_solution(4338474225807303513)
XLA Ops:
  0.0 2.0 %fusion.1 = (f32[3,10,64,16]{3,2,1,0:T(8,128)S(1)}, f32[3,10,64,16]{3,2,1,0:T(8,128)S(1)}) fusion(f32[3,10,64,128]{3,2,1,0:T(8,128)} %tracers.1), kind=kLoop, calls=%fused_computation.3 | loop fusion | bytes 491520 | tf_op jit(solution)/shard_map/slice | solution.py:147
  2.0 0.3 copy.14
  2.3 1.5 %collective-permute-start = (f32[3,10,64,16]{2,3,1,0:T(8,128)S(1)}, f32[3,10,64,16]{2,3,1,0:T(8,128)S(1)}, u32[]{:S(2)}, u32[]{:S(2)}) collective-permute-start(f32[3,10,64,16]{2,3,1,0:T(8,128)S(1)} %copy.14), channel_id=1, source_target_pairs={{2,0},{4,2},{6,4},{8,6},{10,8},{12,10},{14,12},{16,14},{18,16},{20... | collective-permute-start | bytes 368648 | tf_op jit(solution)/shard_map/ppermute | solution.py:19
  3.7 0.3 copy.15
  4.0 1.7 %collective-permute-start.1 = (f32[3,10,64,16]{2,3,1,0:T(8,128)S(1)}, f32[3,10,64,16]{2,3,1,0:T(8,128)S(1)}, u32[]{:S(2)}, u32[]{:S(2)}) collective-permute-start(f32[3,10,64,16]{2,3,1,0:T(8,128)S(1)} %copy.15), channel_id=1, source_target_pairs={{126,0},{0,2},{2,4},{4,6},{6,8},{8,10},{10,12},{12,14},{14,16},{16... | collective-permute-start | bytes 368648 | tf_op jit(solution)/shard_map/ppermute | solution.py:19
  5.7 0.1 pad.1.clone
  5.8 3.4 %collective-permute-done = f32[3,10,64,16]{2,3,1,0:T(8,128)S(1)} collective-permute-done((f32[3,10,64,16]{2,3,1,0:T(8,128)S(1)}, f32[3,10,64,16]{2,3,1,0:T(8,128)S(1)}, u32[]{:S(2)}, u32[]{:S(2)}) %collective-permute-start) | collective-permute-done | bytes 122912 | tf_op jit(solution)/shard_map/ppermute | solution.py:19
  9.2 0.3 copy.11
  9.6 0.0 copy-start
  9.6 0.0 copy-start.1
  9.6 0.0 copy-start.2
  9.6 0.0 copy-start.3
  9.6 0.0 copy-start.4
  9.6 0.0 copy-start.5
  9.6 2.2 %collective-permute-done.1 = f32[3,10,64,16]{2,3,1,0:T(8,128)S(1)} collective-permute-done((f32[3,10,64,16]{2,3,1,0:T(8,128)S(1)}, f32[3,10,64,16]{2,3,1,0:T(8,128)S(1)}, u32[]{:S(2)}, u32[]{:S(2)}) %collective-permute-start.1) | collective-permute-done | bytes 122912 | tf_op jit(solution)/shard_map/ppermute | solution.py:19
  11.8 1.3 %copy.12 = f32[3,10,64,16]{3,2,1,0:T(8,128)} copy(f32[3,10,64,16]{2,3,1,0:T(8,128)S(1)} %collective-permute-done.1) | data formatting | bytes 245760 | tf_op jit(solution)/shard_map/ppermute | solution.py:19
  13.1 1.5 %pad_maximum_fusion.halo = f32[3,10,64,128]{3,2,1,0:T(8,128)S(1)} fusion(f32[3,10,64,16]{3,2,1,0:T(8,128)} %copy.12, f32[3,10,64,16]{3,2,1,0:T(8,128)S(1)} %copy.11, f32[128]{0:T(128)S(1)} %pad.1.clone), kind=kLoop, calls=%fused_computation | loop fusion | flops 491520 | bytes 1229312 | tf_op jit(solution)/shard_map/concatenate | solution.py:149
  14.7 0.0 copy-done
  14.7 0.0 copy-done.1
  14.7 0.0 copy-done.2
  14.7 0.0 copy-done.3
  14.7 0.0 copy-done.4
  14.7 0.0 copy-done.5
  14.7 26.9 %advect_solve_pack.1 = f32[128,32,128]{2,1,0:T(8,128)S(1)} custom-call(f32[3,10,64,128]{3,2,1,0:T(8,128)S(1)} %copy-done, f32[3,10,64,128]{3,2,1,0:T(8,128)S(1)} %pad_maximum_fusion.halo, s32[10,64,128]{2,1,0:T(8,128)S(1)} %copy-done.1, f32[10,64,128]{2,1,0:T(8,128)S(1)} %copy-done.2, f32[9,64,128]{2,1,0:T(8,128)S(1)} %copy-done.3, s32[128,128]{1,0:T(8,128)S(1)} %bitcast.1, ...), custom_call_target="tpu_custom_call" | custom-call | tf_op jit(solution)/shard_map/advect_solve_pack/pallas_call | solution.py:152
  41.7 42.1 %all_to_all.5.arrived = f32[128,32,128]{2,1,0:T(8,128)S(1)} all-to-all(f32[128,32,128]{2,1,0:T(8,128)S(1)} %advect_solve_pack.1), channel_id=1, replica_groups=mesh['lon'=64,'lat'=2] {'lon','lat'}, dimensions={0} | all-to-all | bytes 4194304 | tf_op jit(solution)/shard_map/all_to_all | solution.py:165
  83.7 2.4 %fusion.counts = s32[128]{0:T(128)S(1)} fusion(f32[128,32,128]{2,1,0:T(8,128)S(1)} %all_to_all.5.arrived), kind=kLoop, calls=%fused_computation.2 | loop fusion | flops 128 | bytes 1024 | tf_op jit(solution)/shard_map/convert_element_type | solution.py:166
  86.1 9.8 %place_owned.1 = f32[3,10,8192]{2,1,0:T(8,128)S(1)} custom-call(f32[128,32,128]{2,1,0:T(8,128)S(1)} %all_to_all.5.arrived, s32[128]{0:T(128)S(1)} %fusion.counts), custom_call_target="tpu_custom_call" | custom-call | tf_op jit(solution)/shard_map/place_owned/pallas_call | solution.py:167
  95.9 1.7 %copy.13 = f32[3,10,8192]{2,0,1:T(4,128)} copy(f32[3,10,8192]{2,1,0:T(8,128)S(1)} %place_owned.1) | data formatting | bytes 1966080 | tf_op jit(solution)/shard_map/place_owned/pallas_call | solution.py:167
  (1 shorter events, 0.0 us)
Async XLA Ops:
  2.3 7.0 %collective-permute-start = (f32[3,10,64,16]{2,3,1,0:T(8,128)S(1)}, f32[3,10,64,16]{2,3,1,0:T(8,128)S(1)}, u32[]{:S(2)}, u32[]{:S(2)}) collective-permute-start(f32[3,10,64,16]{2,3,1,0:T(8,128)S(1)} %copy.14), channel_id=1, source_target_pairs={{2,0},{4,2},{6,4},{8,6},{10,8},{12,10},{14,12},{16,14},{18,16},{20... | collective-permute-start | bytes 368648 | tf_op jit(solution)/shard_map/ppermute | solution.py:19
  4.0 7.8 %collective-permute-start.1 = (f32[3,10,64,16]{2,3,1,0:T(8,128)S(1)}, f32[3,10,64,16]{2,3,1,0:T(8,128)S(1)}, u32[]{:S(2)}, u32[]{:S(2)}) collective-permute-start(f32[3,10,64,16]{2,3,1,0:T(8,128)S(1)} %copy.15), channel_id=1, source_target_pairs={{126,0},{0,2},{2,4},{4,6},{6,8},{8,10},{10,12},{12,14},{14,16},{16... | collective-permute-start | bytes 368648 | tf_op jit(solution)/shard_map/ppermute | solution.py:19
  9.6 5.1 %copy-start = (f32[3,10,64,128]{3,2,1,0:T(8,128)S(1)}, f32[3,10,64,128]{3,2,1,0:T(8,128)}, u32[]{:S(2)}) copy-start(f32[3,10,64,128]{3,2,1,0:T(8,128)} %tracers.1) | copy-start | bytes 2949124
  9.6 5.1 %copy-start.1 = (s32[10,64,128]{2,1,0:T(8,128)S(1)}, s32[10,64,128]{2,1,0:T(8,128)}, u32[]{:S(2)}) copy-start(s32[10,64,128]{2,1,0:T(8,128)} %offsets.1) | copy-start | bytes 983044
  9.6 5.1 %copy-start.2 = (f32[10,64,128]{2,1,0:T(8,128)S(1)}, f32[10,64,128]{2,1,0:T(8,128)}, u32[]{:S(2)}) copy-start(f32[10,64,128]{2,1,0:T(8,128)} %weights.1) | copy-start | bytes 983044
  9.6 5.1 %copy-start.3 = (f32[9,64,128]{2,1,0:T(8,128)S(1)}, f32[9,64,128]{2,1,0:T(8,128)}, u32[]{:S(2)}) copy-start(f32[9,64,128]{2,1,0:T(8,128)} %diffusion.1) | copy-start | bytes 884740
  9.6 5.1 %copy-start.4 = (s32[1,128,128]{2,1,0:T(8,128)S(1)}, s32[1,128,128]{2,1,0:T(8,128)}, u32[]{:S(2)}) copy-start(s32[1,128,128]{2,1,0:T(8,128)} %param.10) | copy-start | bytes 196612
  9.6 5.1 %copy-start.5 = (s32[1,128]{1,0:T(1,128)S(1)}, s32[1,128]{1,0:T(1,128)}, u32[]{:S(2)}) copy-start(s32[1,128]{1,0:T(1,128)} %count.1) | copy-start | bytes 1540

commit v2 on v1

v2 whole, which is shorter than its diff:
```python
import jax
import jax.numpy as jnp
from jax import lax
from jax.experimental import pallas as pl
from jax.experimental.pallas import tpu as pltpu
from jax.sharding import PartitionSpec as P

NTR = 3
LEV = 10
HALO = 16
FEAT = 32
SENT = NTR * LEV + 1
LANES = 128
FOUR = LANES // FEAT
EDGES = LANES // HALO
PEERS = 128
AXES = ("lon", "lat")
MESH = pl.DeviceIdType.MESH


def torus_target(lon, lat, shift, flip):
    x, y, z, core = (lon // 8) % 4, lat * 2 + lon // 32, (lon // 2) % 4, lon % 2
    x = (x + shift) % 4
    y = (y + shift // 4 + shift) % 4
    z = (z + shift // 16 + shift // 4 + shift) % 4
    core = (core + flip) % 2
    return (y % 2) * 32 + x * 8 + z * 2 + core, y // 2


def solve_levels(values, coefs):
    upper, reduced = [], [[] for _ in values]
    for level in range(LEV):
        denom = jnp.ones_like(coefs[0])
        if level > 0:
            denom = denom + coefs[level - 1]
        if level < LEV - 1:
            denom = denom + coefs[level]
        if level > 0:
            denom = denom - coefs[level - 1] * upper[level - 1]
        inverse = 1.0 / denom
        if level < LEV - 1:
            upper.append(coefs[level] * inverse)
        for t in range(len(values)):
            right = values[t][level]
            if level > 0:
                right = right + coefs[level - 1] * reduced[t][level - 1]
            reduced[t].append(right * inverse)
    output = [[None] * LEV for _ in values]
    for t in range(len(values)):
        output[t][LEV - 1] = reduced[t][LEV - 1]
        for level in range(LEV - 2, -1, -1):
            output[t][level] = reduced[t][level] + upper[level] * output[t][level + 1]
    return output


def exchange_kernel(
    tracers, offsets, weights, diffusion, index, count, arrived, lengths,
    edge_low, edge_high, from_east, from_west, rows, table, stage, outbox, place, address,
    edge_sems, address_sem, send_sem, recv_sem,
):
    lat_rows = tracers.shape[2]
    groups = lat_rows // 8
    packs = from_east.shape[1]
    lon, lat = lax.axis_index("lon"), lax.axis_index("lat")
    bands = lax.axis_size("lon")
    me = lon * 2 + lat
    lane = lax.broadcasted_iota(jnp.int32, (8, LANES), 1)
    lane_group = lax.broadcasted_iota(jnp.int32, (LANES, LANES), 1) // FEAT

    barrier = pltpu.get_barrier_semaphore()

    def greet(other, carry):
        to_lon, to_lat = torus_target(lon, lat, other // 2, other % 2)
        pl.semaphore_signal(barrier, inc=1, device_id=(to_lon, to_lat), device_id_type=MESH)
        return carry

    lax.fori_loop(1, PEERS, greet, 0)

    def pack_edges(group, carry):
        at = pl.ds(pl.multiple_of(group * 8, 8), 8)
        for pack in range(packs):
            low = high = None
            for part in range(EDGES):
                plane = pack * EDGES + part
                if plane >= NTR * LEV:
                    continue
                value = tracers[plane // LEV, plane % LEV, at, :]
                to_low = pltpu.roll(value, part * HALO, 1) if part else value
                to_high = pltpu.roll(value, (part + 1) * HALO, 1) if part + 1 < EDGES else value
                inside = lane // HALO == part
                low = to_low if part == 0 else jnp.where(inside, to_low, low)
                high = to_high if part == 0 else jnp.where(inside, to_high, high)
            edge_low[group, pack] = low
            edge_high[group, pack] = high
        return carry

    lax.fori_loop(0, groups, pack_edges, 0)

    column = index[...]
    owner = lax.broadcasted_iota(jnp.int32, column.shape, 0)
    member_of = ((owner // 16) % 4 - (lon // 8) % 4 + 4) % 4
    row = column // LANES
    turn_by = (member_of - row % 4 + 4) % 4
    place[...] = turn_by * (lat_rows * LANES // 4) + (row // 4) * LANES + column % LANES
    to_scalars = pltpu.make_async_copy(place, address, address_sem)
    to_scalars.start()

    pl.semaphore_wait(barrier, PEERS - 1)
    to_west = pltpu.make_async_remote_copy(
        src_ref=edge_low, dst_ref=from_east, send_sem=edge_sems.at[0], recv_sem=edge_sems.at[1],
        device_id=(lax.rem(lon + bands - 1, bands), lat), device_id_type=MESH,
    )
    to_east = pltpu.make_async_remote_copy(
        src_ref=edge_high, dst_ref=from_west, send_sem=edge_sems.at[2], recv_sem=edge_sems.at[3],
        device_id=(lax.rem(lon + 1, bands), lat), device_id_type=MESH,
    )
    to_west.start()
    to_east.start()
    to_west.wait()
    to_east.wait()

    def advect_group(group, carry):
        at = pl.ds(pl.multiple_of(group * 8, 8), 8)
        values = [[] for _ in range(NTR)]
        for level in range(LEV):
            cell = lane + offsets[level, at, :]
            weight = weights[level, at, :]
            west_in = (cell >= 0) & (cell < LANES)
            west_at = cell & (LANES - 1)
            east_in = (cell >= -1) & (cell < LANES - 1)
            east_at = (cell + 1) & (LANES - 1)
            for t in range(NTR):
                plane = t * LEV + level
                pack, part = plane // EDGES, plane % EDGES
                main = tracers[t, level, at, :]
                right = from_east[group, pack]
                left = from_west[group, pack]
                if part:
                    right = pltpu.roll(right, LANES - part * HALO, 1)
                if part + 1 < EDGES:
                    left = pltpu.roll(left, LANES - (part + 1) * HALO, 1)
                edge = jnp.where(lane < LANES // 2, right, left)
                west = jnp.where(
                    west_in,
                    jnp.take_along_axis(main, west_at, axis=1),
                    jnp.take_along_axis(edge, west_at, axis=1),
                )
                east = jnp.where(
                    east_in,
                    jnp.take_along_axis(main, east_at, axis=1),
                    jnp.take_along_axis(edge, east_at, axis=1),
                )
                values[t].append((1.0 - weight) * west + weight * east)
        coefs = [diffusion[level, at, :] for level in range(LEV - 1)]
        solved = solve_levels(values, coefs)
        for t in range(NTR):
            for level in range(LEV):
                rows[pl.ds(group * 8 * FEAT + level * NTR + t, 8, stride=FEAT), :] = solved[t][level]
        for spare in range(NTR * LEV, FEAT):
            rows[pl.ds(group * 8 * FEAT + spare, 8, stride=FEAT), :] = jnp.zeros((8, LANES), jnp.float32)
        return carry

    lax.fori_loop(0, groups, advect_group, 0)

    def turn(block, carry):
        at = pl.ds(pl.multiple_of(block * LANES, LANES), LANES)
        turned = rows[at, :].T
        for by in range(FOUR):
            table[by, at, :] = pltpu.roll(turned, by * FEAT, 1) if by else turned
        return carry

    lax.fori_loop(0, lat_rows // FOUR, turn, 0)

    table_rows = table.reshape(FOUR * lat_rows * LANES // FOUR, LANES)

    def send_step(step, carry):
        targets = []
        for member in range(FOUR):
            to_lon, to_lat = torus_target(lon, lat, (step // 2) * FOUR + member, step % 2)
            targets.append((to_lon, to_lat, to_lon * 2 + to_lat))
        for slot in range(LANES):
            for member in range(FOUR):
                at = address[targets[member][2], slot]
                stage[member, slot : slot + 1, :] = table_rows[pl.ds(at, 1), :]
        wide = stage[0]
        for member in range(1, FOUR):
            wide = jnp.where(lane_group == member, stage[member], wide)
        turned = wide.T
        for member in range(FOUR):
            to_lon, to_lat, owner = targets[member]
            box = step * FOUR + member
            outbox[box] = turned[member * FEAT : (member + 1) * FEAT, :]
            length = count[0, owner].astype(jnp.float32)
            outbox[box, SENT - 1 : SENT, :] = jnp.full((1, LANES), length, jnp.float32)
            slot = lax.rem(owner - me + PEERS, PEERS)

            def send():
                pltpu.make_async_remote_copy(
                    src_ref=outbox.at[box, 0:SENT], dst_ref=arrived.at[slot, 0:SENT],
                    send_sem=send_sem, recv_sem=recv_sem,
                    device_id=(to_lon, to_lat), device_id_type=MESH,
                ).start()

            if member:
                send()
            else:
                pl.when(step > 0)(send)
        return carry

    to_scalars.wait()
    lax.fori_loop(0, PEERS // FOUR, send_step, 0)
    arrived[0] = outbox[0]
    others = pltpu.make_async_copy(outbox.at[1:PEERS, 0:SENT], arrived.at[1:PEERS, 0:SENT], recv_sem)
    others.wait()
    pltpu.make_async_copy(outbox.at[1:PEERS, 0:SENT], arrived.at[1:PEERS, 0:SENT], send_sem).wait()
    lengths[...] = arrived[:, SENT - 1, :].T[0:1, :].astype(jnp.int32)


def place_kernel(arrived, lengths, out, owned):
    columns = out.shape[2]
    lane = lax.broadcasted_iota(jnp.int32, (FEAT, LANES), 1)

    def place(source, start):
        block = start // LANES
        shift = lax.rem(start, LANES)
        rolled = pltpu.roll(arrived[source], shift, 1)
        first = pl.ds(pl.multiple_of(block * FEAT, FEAT), FEAT)
        second = pl.ds(pl.multiple_of(block * FEAT + FEAT, FEAT), FEAT)
        pltpu.store(owned.at[first, :], rolled, mask=lane >= shift)
        owned[second, :] = rolled
        return start + lengths[0, source]

    lax.fori_loop(0, arrived.shape[0], place, jnp.int32(0), unroll=4)

    for block in range(columns // LANES):
        for level in range(LEV):
            begin = block * FEAT + level * NTR
            out[level, :, block * LANES : (block + 1) * LANES] = owned[begin : begin + NTR, :]


def body(tracers, offsets, weights, diffusion, send_index, send_count):
    lat_rows, lon_width = tracers.shape[2:]
    columns = lat_rows * lon_width
    groups = lat_rows // 8
    packs = -(-NTR * LEV // EDGES)
    vmem = pl.BlockSpec(memory_space=pltpu.VMEM)
    smem = pl.BlockSpec(memory_space=pltpu.SMEM)
    edge = pltpu.VMEM((groups, packs, 8, LANES), jnp.float32)
    arrived, lengths = pl.pallas_call(
        exchange_kernel,
        out_shape=(
            jax.ShapeDtypeStruct((PEERS, FEAT, LANES), jnp.float32),
            jax.ShapeDtypeStruct((1, PEERS), jnp.int32),
        ),
        in_specs=[vmem] * 5 + [smem],
        out_specs=(vmem, vmem),
        scratch_shapes=[
            edge, edge, edge, edge,
            pltpu.VMEM((lat_rows * FEAT, LANES), jnp.float32),
            pltpu.VMEM((FOUR, columns // FOUR, LANES), jnp.float32),
            pltpu.VMEM((FOUR, LANES, LANES), jnp.float32),
            pltpu.VMEM((PEERS, FEAT, LANES), jnp.float32),
            pltpu.VMEM((PEERS, LANES), jnp.int32),
            pltpu.SMEM((PEERS, LANES), jnp.int32),
            pltpu.SemaphoreType.DMA((4,)),
            pltpu.SemaphoreType.DMA,
            pltpu.SemaphoreType.DMA,
            pltpu.SemaphoreType.DMA,
        ],
        compiler_params=pltpu.CompilerParams(vmem_limit_bytes=40 << 20, collective_id=0, has_side_effects=True),
        name="advect_solve_exchange",
    )(tracers, offsets, weights, diffusion, send_index[0], send_count)
    owned = pl.pallas_call(
        place_kernel,
        out_shape=jax.ShapeDtypeStruct((LEV, NTR, columns), jnp.float32),
        in_specs=[vmem, smem],
        out_specs=vmem,
        scratch_shapes=[pltpu.VMEM(((columns // LANES + 2) * FEAT, LANES), jnp.float32)],
        compiler_params=pltpu.CompilerParams(vmem_limit_bytes=32 << 20),
        name="place_owned",
    )(arrived, lengths)
    return jnp.transpose(owned, (1, 0, 2))


def solution(mesh):
    return jax.shard_map(
        body,
        mesh=mesh,
        in_specs=(
            P(None, None, "lat", "lon"),
            P(None, "lat", "lon"),
            P(None, "lat", "lon"),
            P(None, "lat", "lon"),
            P(("lon", "lat"), None, None),
            P(("lon", "lat"), None),
        ),
        out_specs=P(None, None, ("lon", "lat")),
        check_vma=False,
    )
```

time: 97.8 us -> 71.2 us (0.73)
  blocking collectives: 42.1 us -> 0 us
  Pallas kernels: 36.8 us -> 65.3 us
  waiting for transfers between devices: 5.67 us -> 0 us
  other arithmetic: 3.88 us -> 0 us
  starting transfers between devices: 3.14 us -> 0 us
    all_to_all x1 -> x0, blocking collectives: 42.1 us -> none  [body(): lax.all_to_all(packed, AXES, split_axis=0, concat_axis=0, tiled=True)]
    pallas_call x2, Pallas kernels: 36.8 us -> 65.3 us  [the longest x1 60.7 us: body(): pl.pallas_call(exchange_kernel, out_shape=(jax.ShapeDtypeStruct((PEERS, F...]
    ppermute x2 -> x0, waiting for transfers between devices: 5.67 us -> none  [shifted(): return lax.ppermute(block, axis, route)]
    unnamed x14 -> x12, local copies, waits for them, and re-layouts: 0.64 us -> 5.6 us
    ppermute x2 -> x0, starting transfers between devices: 3.14 us -> none  [shifted(): return lax.ppermute(block, axis, route)]
    convert_element_type x1 -> x0, other arithmetic: 2.36 us -> none  [body(): counts = arrived[:, NTR * LEV, 0].astype(jnp.int32)]
    slice x1 -> x0, local copies, waits for them, and re-layouts: 1.95 us -> none  [body(): from_east = shifted(tracers[..., :HALO], 'lon', -1)]
    pallas_call x1 -> x0, local copies, waits for them, and re-layouts: 1.73 us -> none  [body(): pl.pallas_call(place_kernel, out_shape=jax.ShapeDtypeStruct((NTR, LEV, co...]
  transfers between devices with their start and end apart: 2 -> 0, of which waited for: 2 -> 0; matrix products, arithmetic and copies ran while one was open for 1% -> 0% of each run, Pallas kernels for 0% -> 0%
where the time goes in v2:
time: 71.2 us; the launch traced here: 70.9 us
  Pallas kernels  65.3 us (92%)
  local copies, waits for them, and re-layouts  5.6 us (8%)
    pallas_call x1, Pallas kernels, body(): pl.pallas_call(exchange_kernel, out_shape=(jax.ShapeDtypeStruct((PEERS, F...  60.7 us
    unnamed x12, local copies, waits for them, and re-layouts  5.6 us
    pallas_call x1, Pallas kernels, body(): pl.pallas_call(place_kernel, out_shape=jax.ShapeDtypeStruct((LEV, NTR, co...  4.59 us

profile of v2, /device:TPU:1, one launch (start us, length us, event | category | flops | bytes accessed | tf_op | source)
XLA Modules:
  0.0 70.9 jit_solution(15796329964417988917)
XLA Ops:
  0.0 0.0 copy-start
  0.0 1.2 %copy-done = f32[3,10,64,128]{3,2,1,0:T(8,128)S(1)} copy-done((f32[3,10,64,128]{3,2,1,0:T(8,128)S(1)}, f32[3,10,64,128]{3,2,1,0:T(8,128)}, u32[]{:S(2)}) %copy-start) | copy-done | bytes 983064
  1.2 0.0 copy-start.1
  1.2 1.0 %copy-done.1 = s32[10,64,128]{2,1,0:T(8,128)S(1)} copy-done((s32[10,64,128]{2,1,0:T(8,128)S(1)}, s32[10,64,128]{2,1,0:T(8,128)}, u32[]{:S(2)}) %copy-start.1) | copy-done | bytes 327704
  2.2 0.0 copy-start.2
  2.2 1.0 %copy-done.2 = f32[10,64,128]{2,1,0:T(8,128)S(1)} copy-done((f32[10,64,128]{2,1,0:T(8,128)S(1)}, f32[10,64,128]{2,1,0:T(8,128)}, u32[]{:S(2)}) %copy-start.2) | copy-done | bytes 327704
  3.1 0.0 copy-start.3
  3.2 1.0 %copy-done.3 = f32[9,64,128]{2,1,0:T(8,128)S(1)} copy-done((f32[9,64,128]{2,1,0:T(8,128)S(1)}, f32[9,64,128]{2,1,0:T(8,128)}, u32[]{:S(2)}) %copy-start.3) | copy-done | bytes 294936
  4.1 0.0 copy-start.4
  4.1 0.8 %copy-done.4 = s32[1,128,128]{2,1,0:T(8,128)S(1)} copy-done((s32[1,128,128]{2,1,0:T(8,128)S(1)}, s32[1,128,128]{2,1,0:T(8,128)}, u32[]{:S(2)}) %copy-start.4) | copy-done | bytes 65560
  5.0 0.0 copy-start.5
  5.0 0.7 copy-done.5
  5.6 60.7 %advect_solve_exchange.1 = (f32[128,32,128]{2,1,0:T(8,128)S(1)}, s32[1,128]{1,0:T(1,128)S(1)}) custom-call(f32[3,10,64,128]{3,2,1,0:T(8,128)S(1)} %copy-done, s32[10,64,128]{2,1,0:T(8,128)S(1)} %copy-done.1, f32[10,64,128]{2,1,0:T(8,128)S(1)} %copy-done.2, f32[9,64,128]{2,1,0:T(8,128)S(1)} %copy-done.3, s32[128,128]{1,0:T(8,128)S(1)} %bitcast.2, ...), custom_call_target="tpu_custom_call" | custom-call | tf_op jit(solution)/shard_map/advect_solve_exchange/pallas_call | solution.py:249
  66.4 4.6 %place_owned.1 = f32[10,3,8192]{2,1,0:T(4,128)} custom-call(f32[128,32,128]{2,1,0:T(8,128)S(1)} %get-tuple-element.7.arrived, s32[1,128]{1,0:T(1,128)S(1)} %get-tuple-element.8.lengths), custom_call_target="tpu_custom_call" | custom-call | tf_op jit(solution)/shard_map/place_owned/pallas_call | solution.py:273
Async XLA Ops:
  0.0 1.2 %copy-start = (f32[3,10,64,128]{3,2,1,0:T(8,128)S(1)}, f32[3,10,64,128]{3,2,1,0:T(8,128)}, u32[]{:S(2)}) copy-start(f32[3,10,64,128]{3,2,1,0:T(8,128)} %tracers.1) | copy-start | bytes 2949124
  1.2 1.0 %copy-start.1 = (s32[10,64,128]{2,1,0:T(8,128)S(1)}, s32[10,64,128]{2,1,0:T(8,128)}, u32[]{:S(2)}) copy-start(s32[10,64,128]{2,1,0:T(8,128)} %offsets.1) | copy-start | bytes 983044
  2.2 1.0 %copy-start.2 = (f32[10,64,128]{2,1,0:T(8,128)S(1)}, f32[10,64,128]{2,1,0:T(8,128)}, u32[]{:S(2)}) copy-start(f32[10,64,128]{2,1,0:T(8,128)} %weights.1) | copy-start | bytes 983044
  3.1 1.0 %copy-start.3 = (f32[9,64,128]{2,1,0:T(8,128)S(1)}, f32[9,64,128]{2,1,0:T(8,128)}, u32[]{:S(2)}) copy-start(f32[9,64,128]{2,1,0:T(8,128)} %diffusion.1) | copy-start | bytes 884740
  4.1 0.8 %copy-start.4 = (s32[1,128,128]{2,1,0:T(8,128)S(1)}, s32[1,128,128]{2,1,0:T(8,128)}, u32[]{:S(2)}) copy-start(s32[1,128,128]{2,1,0:T(8,128)} %param.10) | copy-start | bytes 196612
  5.0 0.7 copy-start.5

commit v3 on v2

--- a/solution.py
+++ b/solution.py
@@ -14,6 +14,7 @@
 FOUR = LANES // FEAT
 EDGES = LANES // HALO
 PEERS = 128
+ROW = 16
 AXES = ("lon", "lat")
 MESH = pl.DeviceIdType.MESH
 
@@ -27,8 +28,8 @@
     return (y % 2) * 32 + x * 8 + z * 2 + core, y // 2
 
 
-def solve_levels(values, coefs):
-    upper, reduced = [], [[] for _ in values]
+def factor_levels(coefs):
+    inverses, uppers = [], []
     for level in range(LEV):
         denom = jnp.ones_like(coefs[0])
         if level > 0:
@@ -36,28 +37,40 @@
         if level < LEV - 1:
             denom = denom + coefs[level]
         if level > 0:
-            denom = denom - coefs[level - 1] * upper[level - 1]
-        inverse = 1.0 / denom
+            denom = denom - coefs[level - 1] * uppers[level - 1]
+        inverses.append(1.0 / denom)
         if level < LEV - 1:
-            upper.append(coefs[level] * inverse)
-        for t in range(len(values)):
-            right = values[t][level]
-            if level > 0:
-                right = right + coefs[level - 1] * reduced[t][level - 1]
-            reduced[t].append(right * inverse)
-    output = [[None] * LEV for _ in values]
-    for t in range(len(values)):
-        output[t][LEV - 1] = reduced[t][LEV - 1]
-        for level in range(LEV - 2, -1, -1):
-            output[t][level] = reduced[t][level] + upper[level] * output[t][level + 1]
+            uppers.append(coefs[level] * inverses[level])
+    return inverses, uppers
+
+
+def solve_levels(values, coefs, inverses, uppers):
+    reduced = []
+    for level in range(LEV):
+        right = values[level]
+        if level > 0:
+            right = right + coefs[level - 1] * reduced[level - 1]
+        reduced.append(right * inverses[level])
+    output = [None] * LEV
+    output[LEV - 1] = reduced[LEV - 1]
+    for level in range(LEV - 2, -1, -1):
+        output[level] = reduced[level] + uppers[level] * output[level + 1]
     return output
 
 
 def exchange_kernel(
-    tracers, offsets, weights, diffusion, index, count, arrived, lengths,
+    tracers_hbm, offsets_hbm, weights_hbm, diffusion_hbm, index_hbm, count_hbm, arrived, lengths,
+    tracers, offsets, weights, diffusion, index, count, partial, factors,
     edge_low, edge_high, from_east, from_west, rows, table, stage, outbox, place, address,
-    edge_sems, address_sem, send_sem, recv_sem,
+    load_sems, edge_sems, address_sem, send_sem, recv_sem, ready,
 ):
+    pairs = (
+        (tracers_hbm, tracers), (index_hbm, index), (offsets_hbm, offsets),
+        (weights_hbm, weights), (diffusion_hbm, diffusion), (count_hbm, count),
+    )
+    loads = [pltpu.make_async_copy(source, here, load_sems.at[i]) for i, (source, here) in enumerate(pairs)]
+    for load in loads:
+        load.start()
     lat_rows = tracers.shape[2]
     groups = lat_rows // 8
     packs = from_east.shape[1]
@@ -69,12 +82,19 @@
 
     barrier = pltpu.get_barrier_semaphore()
 
-    def greet(other, carry):
-        to_lon, to_lat = torus_target(lon, lat, other // 2, other % 2)
-        pl.semaphore_signal(barrier, inc=1, device_id=(to_lon, to_lat), device_id_type=MESH)
-        return carry
-
-    lax.fori_loop(1, PEERS, greet, 0)
+    row_first, in_row = (me // ROW) * ROW, lax.rem(me, ROW)
+
+    def greet(semaphore, other):
+        pl.semaphore_signal(semaphore, inc=1, device_id=(other // 2, lax.rem(other, 2)), device_id_type=MESH)
+
+    for ring in (2, PEERS - 2):
+        greet(barrier, lax.rem(me + ring, PEERS))
+    for step in range(1, ROW):
+        greet(barrier, row_first + lax.rem(in_row + step, ROW))
+    for step in range(ROW, PEERS, ROW):
+        greet(barrier, lax.rem(me + step, PEERS))
+
+    loads[0].wait()
 
     def pack_edges(group, carry):
         at = pl.ds(pl.multiple_of(group * 8, 8), 8)
@@ -85,27 +105,18 @@
                 if plane >= NTR * LEV:
                     continue
                 value = tracers[plane // LEV, plane % LEV, at, :]
-                to_low = pltpu.roll(value, part * HALO, 1) if part else value
+                low_at = (part + EDGES // 2) % EDGES
+                to_low = pltpu.roll(value, low_at * HALO, 1) if low_at else value
                 to_high = pltpu.roll(value, (part + 1) * HALO, 1) if part + 1 < EDGES else value
-                inside = lane // HALO == part
-                low = to_low if part == 0 else jnp.where(inside, to_low, low)
-                high = to_high if part == 0 else jnp.where(inside, to_high, high)
+                low = to_low if part == 0 else jnp.where(lane // HALO == low_at, to_low, low)
+                high = to_high if part == 0 else jnp.where(lane // HALO == part, to_high, high)
             edge_low[group, pack] = low
             edge_high[group, pack] = high
         return carry
 
     lax.fori_loop(0, groups, pack_edges, 0)
 
-    column = index[...]
-    owner = lax.broadcasted_iota(jnp.int32, column.shape, 0)
-    member_of = ((owner // 16) % 4 - (lon // 8) % 4 + 4) % 4
-    row = column // LANES
-    turn_by = (member_of - row % 4 + 4) % 4
-    place[...] = turn_by * (lat_rows * LANES // 4) + (row // 4) * LANES + column % LANES
-    to_scalars = pltpu.make_async_copy(place, address, address_sem)
-    to_scalars.start()
-
-    pl.semaphore_wait(barrier, PEERS - 1)
+    pl.semaphore_wait(barrier, 2 + ROW - 1 + PEERS // ROW - 1)
     to_west = pltpu.make_async_remote_copy(
         src_ref=edge_low, dst_ref=from_east, send_sem=edge_sems.at[0], recv_sem=edge_sems.at[1],
         device_id=(lax.rem(lon + bands - 1, bands), lat), device_id_type=MESH,
@@ -116,51 +127,76 @@
     )
     to_west.start()
     to_east.start()
-    to_west.wait()
-    to_east.wait()
-
-    def advect_group(group, carry):
+    for step in range(1, ROW):
+        greet(ready, row_first + lax.rem(in_row + step, ROW))
+
+    loads[1].wait()
+    column = index[...]
+    owner = lax.broadcasted_iota(jnp.int32, column.shape, 0)
+    member_of = ((owner // 16) % 4 - (lon // 8) % 4 + 4) % 4
+    row = column // LANES
+    turn_by = (member_of - row % 4 + 4) % 4
+    place[...] = turn_by * (lat_rows * LANES // 4) + (row // 4) * LANES + column % LANES
+    to_scalars = pltpu.make_async_copy(place, address, address_sem)
+    to_scalars.start()
+
+    for load in loads[2:]:
+        load.wait()
+
+    def interior(group, carry):
         at = pl.ds(pl.multiple_of(group * 8, 8), 8)
-        values = [[] for _ in range(NTR)]
         for level in range(LEV):
             cell = lane + offsets[level, at, :]
             weight = weights[level, at, :]
-            west_in = (cell >= 0) & (cell < LANES)
+            west_weight = jnp.where((cell >= 0) & (cell < LANES), 1.0 - weight, 0.0)
+            east_weight = jnp.where((cell >= -1) & (cell < LANES - 1), weight, 0.0)
             west_at = cell & (LANES - 1)
-            east_in = (cell >= -1) & (cell < LANES - 1)
             east_at = (cell + 1) & (LANES - 1)
+            for t in range(NTR):
+                main = tracers[t, level, at, :]
+                west = jnp.take_along_axis(main, west_at, axis=1)
+                east = jnp.take_along_axis(main, east_at, axis=1)
+                partial[t, level, at, :] = west_weight * west + east_weight * east
+        inverses, uppers = factor_levels([diffusion[level, at, :] for level in range(LEV - 1)])
+        for level in range(LEV):
+            factors[level, at, :] = inverses[level]
+        for level in range(LEV - 1):
+            factors[LEV + level, at, :] = uppers[level]
+        return carry
+
+    lax.fori_loop(0, groups, interior, 0)
+    to_west.wait()
+    to_east.wait()
+
+    def finish(group, carry):
+        at = pl.ds(pl.multiple_of(group * 8, 8), 8)
+        values = [[None] * LEV for _ in range(NTR)]
+        for level in range(LEV):
+            cell = lane + offsets[level, at, :]
+            weight = weights[level, at, :]
+            west_weight = jnp.where((cell >= 0) & (cell < LANES), 0.0, 1.0 - weight)
+            east_weight = jnp.where((cell >= -1) & (cell < LANES - 1), 0.0, weight)
+            west_at = (cell & (HALO - 1)) + jnp.where(cell < 0, 0, LANES // 2)
+            east_at = ((cell + 1) & (HALO - 1)) + jnp.where(cell < -1, 0, LANES // 2)
             for t in range(NTR):
                 plane = t * LEV + level
                 pack, part = plane // EDGES, plane % EDGES
-                main = tracers[t, level, at, :]
-                right = from_east[group, pack]
-                left = from_west[group, pack]
-                if part:
-                    right = pltpu.roll(right, LANES - part * HALO, 1)
-                if part + 1 < EDGES:
-                    left = pltpu.roll(left, LANES - (part + 1) * HALO, 1)
-                edge = jnp.where(lane < LANES // 2, right, left)
-                west = jnp.where(
-                    west_in,
-                    jnp.take_along_axis(main, west_at, axis=1),
-                    jnp.take_along_axis(edge, west_at, axis=1),
-                )
-                east = jnp.where(
-                    east_in,
-                    jnp.take_along_axis(main, east_at, axis=1),
-                    jnp.take_along_axis(edge, east_at, axis=1),
-                )
-                values[t].append((1.0 - weight) * west + weight * east)
+                edge = jnp.where(lane // HALO == part, from_west[group, pack], from_east[group, pack])
+                west = jnp.take_along_axis(edge, (west_at + part * HALO) & (LANES - 1), axis=1)
+                east = jnp.take_along_axis(edge, (east_at + part * HALO) & (LANES - 1), axis=1)
+                values[t][level] = partial[t, level, at, :] + (west_weight * west + east_weight * east)
         coefs = [diffusion[level, at, :] for level in range(LEV - 1)]
-        solved = solve_levels(values, coefs)
+        inverses = [factors[level, at, :] for level in range(LEV)]
+        uppers = [factors[LEV + level, at, :] for level in range(LEV - 1)]
         for t in range(NTR):
+            solved = solve_levels(values[t], coefs, inverses, uppers)
             for level in range(LEV):
-                rows[pl.ds(group * 8 * FEAT + level * NTR + t, 8, stride=FEAT), :] = solved[t][level]
+                rows[pl.ds(group * 8 * FEAT + level * NTR + t, 8, stride=FEAT), :] = solved[level]
         for spare in range(NTR * LEV, FEAT):
             rows[pl.ds(group * 8 * FEAT + spare, 8, stride=FEAT), :] = jnp.zeros((8, LANES), jnp.float32)
         return carry
 
-    lax.fori_loop(0, groups, advect_group, 0)
+    lax.fori_loop(0, groups, finish, 0)
 
     def turn(block, carry):
         at = pl.ds(pl.multiple_of(block * LANES, LANES), LANES)
@@ -208,6 +244,7 @@
         return carry
 
     to_scalars.wait()
+    pl.semaphore_wait(ready, ROW - 1)
     lax.fori_loop(0, PEERS // FOUR, send_step, 0)
     arrived[0] = outbox[0]
     others = pltpu.make_async_copy(outbox.at[1:PEERS, 0:SENT], arrived.at[1:PEERS, 0:SENT], recv_sem)
@@ -252,9 +289,17 @@
             jax.ShapeDtypeStruct((PEERS, FEAT, LANES), jnp.float32),
             jax.ShapeDtypeStruct((1, PEERS), jnp.int32),
         ),
-        in_specs=[vmem] * 5 + [smem],
+        in_specs=[pl.BlockSpec(memory_space=pltpu.HBM)] * 6,
         out_specs=(vmem, vmem),
         scratch_shapes=[
+            pltpu.VMEM(tracers.shape, jnp.float32),
+            pltpu.VMEM(offsets.shape, jnp.int32),
+            pltpu.VMEM(weights.shape, jnp.float32),
+            pltpu.VMEM(diffusion.shape, jnp.float32),
+            pltpu.VMEM((PEERS, LANES), jnp.int32),
+            pltpu.SMEM((1, PEERS), jnp.int32),
+            pltpu.VMEM(tracers.shape, jnp.float32),
+            pltpu.VMEM((2 * LEV - 1, lat_rows, lon_width), jnp.float32),
             edge, edge, edge, edge,
             pltpu.VMEM((lat_rows * FEAT, LANES), jnp.float32),
             pltpu.VMEM((FOUR, columns // FOUR, LANES), jnp.float32),
@@ -262,12 +307,14 @@
             pltpu.VMEM((PEERS, FEAT, LANES), jnp.float32),
             pltpu.VMEM((PEERS, LANES), jnp.int32),
             pltpu.SMEM((PEERS, LANES), jnp.int32),
+            pltpu.SemaphoreType.DMA((6,)),
             pltpu.SemaphoreType.DMA((4,)),
             pltpu.SemaphoreType.DMA,
             pltpu.SemaphoreType.DMA,
             pltpu.SemaphoreType.DMA,
+            pltpu.SemaphoreType.REGULAR,
         ],
-        compiler_params=pltpu.CompilerParams(vmem_limit_bytes=40 << 20, collective_id=0, has_side_effects=True),
+        compiler_params=pltpu.CompilerParams(vmem_limit_bytes=66800000, collective_id=0, has_side_effects=True),
         name="advect_solve_exchange",
     )(tracers, offsets, weights, diffusion, send_index[0], send_count)
     owned = pl.pallas_call(

time: 71.2 us -> 53.8 us (0.76)
  Pallas kernels: 65.3 us -> 51.5 us
  local copies, waits for them, and re-layouts: 5.6 us -> 2.16 us
    pallas_call x1, Pallas kernels: 60.7 us -> 46.9 us  [body(): pl.pallas_call(exchange_kernel, out_shape=(jax.ShapeDtypeStruct((PEERS, F...]
    unnamed x12 -> x4, local copies, waits for them, and re-layouts: 5.6 us -> 2.16 us
where the time goes in v3:
time: 53.8 us; the launch traced here: 53.7 us
  Pallas kernels  51.5 us (96%)
  local copies, waits for them, and re-layouts  2.16 us (4%)
    pallas_call x1, Pallas kernels, body(): pl.pallas_call(exchange_kernel, out_shape=(jax.ShapeDtypeStruct((PEERS, F...  46.9 us
    pallas_call x1, Pallas kernels, body(): pl.pallas_call(place_kernel, out_shape=jax.ShapeDtypeStruct((LEV, NTR, co...  4.59 us
    unnamed x4, local copies, waits for them, and re-layouts  2.16 us

profile of v3, /device:TPU:1, one launch (start us, length us, event | category | flops | bytes accessed | tf_op | source)
XLA Modules:
  0.0 53.7 jit_solution(2846185755880280176)
XLA Ops:
  0.0 46.9 %advect_solve_exchange.1 = (f32[128,32,128]{2,1,0:T(8,128)}, s32[1,128]{1,0:T(1,128)}) custom-call(f32[3,10,64,128]{3,2,1,0:T(8,128)} %tracers_hbm.1, s32[10,64,128]{2,1,0:T(8,128)} %offsets_hbm.1, f32[10,64,128]{2,1,0:T(8,128)} %weights_hbm.1, f32[9,64,128]{2,1,0:T(8,128)} %diffusion_hbm.1, s32[128,128]{1,0:T(8,128)} %bitcast.2, s32[1,128]{1,0:T(1,128)} %count_hbm.1), custom_call_target="tpu_custom_call" | custom-call | tf_op jit(solution)/shard_map/advect_solve_exchange/pallas_call | solution.py:286
  46.9 0.0 copy-start
  46.9 1.6 %copy-done = f32[128,32,128]{2,1,0:T(8,128)S(1)} copy-done((f32[128,32,128]{2,1,0:T(8,128)S(1)}, f32[128,32,128]{2,1,0:T(8,128)}, u32[]{:S(2)}) %copy-start) | copy-done | bytes 2097176
  48.5 0.0 copy-start.1
  48.5 0.6 %copy-done.1 = s32[1,128]{1,0:T(1,128)S(1)} copy-done((s32[1,128]{1,0:T(1,128)S(1)}, s32[1,128]{1,0:T(1,128)}, u32[]{:S(2)}) %copy-start.1) | copy-done | bytes 536
  49.1 4.6 %place_owned.1 = f32[10,3,8192]{2,1,0:T(4,128)} custom-call(f32[128,32,128]{2,1,0:T(8,128)S(1)} %copy-done, s32[1,128]{1,0:T(1,128)S(1)} %copy-done.1), custom_call_target="tpu_custom_call" | custom-call | tf_op jit(solution)/shard_map/place_owned/pallas_call | solution.py:320
Async XLA Ops:
  46.9 1.6 %copy-start = (f32[128,32,128]{2,1,0:T(8,128)S(1)}, f32[128,32,128]{2,1,0:T(8,128)}, u32[]{:S(2)}) copy-start(f32[128,32,128]{2,1,0:T(8,128)} %get-tuple-element.7.arrived) | copy-start | bytes 6291460
  48.5 0.6 %copy-start.1 = (s32[1,128]{1,0:T(1,128)S(1)}, s32[1,128]{1,0:T(1,128)}, u32[]{:S(2)}) copy-start(s32[1,128]{1,0:T(1,128)} %get-tuple-element.8.lengths) | copy-start | bytes 1540

commit v4 on v3

--- a/solution.py
+++ b/solution.py
@@ -15,6 +15,8 @@
 EDGES = LANES // HALO
 PEERS = 128
 ROW = 16
+PIECE = 2
+OUT_PIECES = 4
 AXES = ("lon", "lat")
 MESH = pl.DeviceIdType.MESH
 
@@ -114,19 +116,24 @@
             edge_high[group, pack] = high
         return carry
 
-    lax.fori_loop(0, groups, pack_edges, 0)
-
-    pl.semaphore_wait(barrier, 2 + ROW - 1 + PEERS // ROW - 1)
-    to_west = pltpu.make_async_remote_copy(
-        src_ref=edge_low, dst_ref=from_east, send_sem=edge_sems.at[0], recv_sem=edge_sems.at[1],
-        device_id=(lax.rem(lon + bands - 1, bands), lat), device_id_type=MESH,
-    )
-    to_east = pltpu.make_async_remote_copy(
-        src_ref=edge_high, dst_ref=from_west, send_sem=edge_sems.at[2], recv_sem=edge_sems.at[3],
-        device_id=(lax.rem(lon + 1, bands), lat), device_id_type=MESH,
-    )
-    to_west.start()
-    to_east.start()
+    def edge_copies(piece):
+        part = pl.ds(piece * PIECE, PIECE)
+        return [
+            pltpu.make_async_remote_copy(
+                src_ref=source.at[part], dst_ref=target.at[part],
+                send_sem=edge_sems.at[side, 0, piece], recv_sem=edge_sems.at[side, 1, piece],
+                device_id=(lax.rem(lon + distance, bands), lat), device_id_type=MESH,
+            )
+            for side, source, target, distance in ((0, edge_low, from_east, bands - 1), (1, edge_high, from_west, 1))
+        ]
+
+    pieces = groups // PIECE
+    for piece in range(pieces):
+        lax.fori_loop(piece * PIECE, piece * PIECE + PIECE, pack_edges, 0, unroll=True)
+        if piece == 0:
+            pl.semaphore_wait(barrier, 2 + ROW - 1 + PEERS // ROW - 1)
+        for copy in edge_copies(piece):
+            copy.start()
     for step in range(1, ROW):
         greet(ready, row_first + lax.rem(in_row + step, ROW))
 
@@ -165,8 +172,6 @@
         return carry
 
     lax.fori_loop(0, groups, interior, 0)
-    to_west.wait()
-    to_east.wait()
 
     def finish(group, carry):
         at = pl.ds(pl.multiple_of(group * 8, 8), 8)
@@ -196,8 +201,6 @@
             rows[pl.ds(group * 8 * FEAT + spare, 8, stride=FEAT), :] = jnp.zeros((8, LANES), jnp.float32)
         return carry
 
-    lax.fori_loop(0, groups, finish, 0)
-
     def turn(block, carry):
         at = pl.ds(pl.multiple_of(block * LANES, LANES), LANES)
         turned = rows[at, :].T
@@ -205,55 +208,78 @@
             table[by, at, :] = pltpu.roll(turned, by * FEAT, 1) if by else turned
         return carry
 
-    lax.fori_loop(0, lat_rows // FOUR, turn, 0)
+    def finish_piece(piece, carry):
+        for copy in edge_copies(piece):
+            copy.wait_recv()
+        lax.fori_loop(piece * PIECE, piece * PIECE + PIECE, finish, 0)
+        blocks = PIECE * 8 // FOUR
+        for block in range(blocks):
+            turn(piece * blocks + block, 0)
+        return carry
+
+    lax.fori_loop(0, pieces, finish_piece, 0)
 
     table_rows = table.reshape(FOUR * lat_rows * LANES // FOUR, LANES)
 
-    def send_step(step, carry):
+    def targets_of(step):
         targets = []
         for member in range(FOUR):
             to_lon, to_lat = torus_target(lon, lat, (step // 2) * FOUR + member, step % 2)
             targets.append((to_lon, to_lat, to_lon * 2 + to_lat))
+        return targets
+
+    def gather(step, half):
+        owners = [owner for _, _, owner in targets_of(step)]
         for slot in range(LANES):
             for member in range(FOUR):
-                at = address[targets[member][2], slot]
-                stage[member, slot : slot + 1, :] = table_rows[pl.ds(at, 1), :]
-        wide = stage[0]
+                at = address[owners[member], slot]
+                stage[half, member, slot : slot + 1, :] = table_rows[pl.ds(at, 1), :]
+
+    def send(step, half, first=0):
+        wide = stage[half, 0]
         for member in range(1, FOUR):
-            wide = jnp.where(lane_group == member, stage[member], wide)
+            wide = jnp.where(lane_group == member, stage[half, member], wide)
         turned = wide.T
-        for member in range(FOUR):
-            to_lon, to_lat, owner = targets[member]
+        for member, (to_lon, to_lat, owner) in enumerate(targets_of(step)):
             box = step * FOUR + member
             outbox[box] = turned[member * FEAT : (member + 1) * FEAT, :]
             length = count[0, owner].astype(jnp.float32)
             outbox[box, SENT - 1 : SENT, :] = jnp.full((1, LANES), length, jnp.float32)
             slot = lax.rem(owner - me + PEERS, PEERS)
-
-            def send():
+            if member >= first:
                 pltpu.make_async_remote_copy(
                     src_ref=outbox.at[box, 0:SENT], dst_ref=arrived.at[slot, 0:SENT],
                     send_sem=send_sem, recv_sem=recv_sem,
                     device_id=(to_lon, to_lat), device_id_type=MESH,
                 ).start()
 
-            if member:
-                send()
-            else:
-                pl.when(step > 0)(send)
-        return carry
-
     to_scalars.wait()
     pl.semaphore_wait(ready, ROW - 1)
-    lax.fori_loop(0, PEERS // FOUR, send_step, 0)
+    steps = PEERS // FOUR
+    gather(0, 0)
+    send(0, 0, first=1)
+    gather(1, 1)
+
+    def two_steps(turn_at, carry):
+        send(2 * turn_at + 1, 1)
+        gather(2 * turn_at + 2, 0)
+        send(2 * turn_at + 2, 0)
+        gather(2 * turn_at + 3, 1)
+        return carry
+
+    lax.fori_loop(0, steps // 2 - 1, two_steps, 0)
+    send(steps - 1, 1)
     arrived[0] = outbox[0]
     others = pltpu.make_async_copy(outbox.at[1:PEERS, 0:SENT], arrived.at[1:PEERS, 0:SENT], recv_sem)
     others.wait()
     pltpu.make_async_copy(outbox.at[1:PEERS, 0:SENT], arrived.at[1:PEERS, 0:SENT], send_sem).wait()
     lengths[...] = arrived[:, SENT - 1, :].T[0:1, :].astype(jnp.int32)
-
-
-def place_kernel(arrived, lengths, out, owned):
+    for piece in range(pieces):
+        for copy in edge_copies(piece):
+            copy.wait_send()
+
+
+def place_kernel(arrived, lengths, out, owned, rows, out_sems):
     columns = out.shape[2]
     lane = lax.broadcasted_iota(jnp.int32, (FEAT, LANES), 1)
 
@@ -267,12 +293,20 @@
         owned[second, :] = rolled
         return start + lengths[0, source]
 
-    lax.fori_loop(0, arrived.shape[0], place, jnp.int32(0), unroll=4)
-
-    for block in range(columns // LANES):
-        for level in range(LEV):
-            begin = block * FEAT + level * NTR
-            out[level, :, block * LANES : (block + 1) * LANES] = owned[begin : begin + NTR, :]
+    lax.fori_loop(0, arrived.shape[0], place, jnp.int32(0), unroll=16)
+
+    copies = []
+    width = columns // OUT_PIECES
+    for piece in range(OUT_PIECES):
+        for block in range(piece * width // LANES, (piece + 1) * width // LANES):
+            for level in range(LEV):
+                begin = block * FEAT + level * NTR
+                rows[level, :, block * LANES : (block + 1) * LANES] = owned[begin : begin + NTR, :]
+        part = pl.ds(piece * width, width)
+        copies.append(pltpu.make_async_copy(rows.at[:, :, part], out.at[:, :, part], out_sems.at[piece]))
+        copies[-1].start()
+    for copy in copies:
+        copy.wait()
 
 
 def body(tracers, offsets, weights, diffusion, send_index, send_count):
@@ -303,26 +337,30 @@
             edge, edge, edge, edge,
             pltpu.VMEM((lat_rows * FEAT, LANES), jnp.float32),
             pltpu.VMEM((FOUR, columns // FOUR, LANES), jnp.float32),
-            pltpu.VMEM((FOUR, LANES, LANES), jnp.float32),
+            pltpu.VMEM((2, FOUR, LANES, LANES), jnp.float32),
             pltpu.VMEM((PEERS, FEAT, LANES), jnp.float32),
             pltpu.VMEM((PEERS, LANES), jnp.int32),
             pltpu.SMEM((PEERS, LANES), jnp.int32),
             pltpu.SemaphoreType.DMA((6,)),
-            pltpu.SemaphoreType.DMA((4,)),
+            pltpu.SemaphoreType.DMA((2, 2, groups // PIECE)),
             pltpu.SemaphoreType.DMA,
             pltpu.SemaphoreType.DMA,
             pltpu.SemaphoreType.DMA,
             pltpu.SemaphoreType.REGULAR,
         ],
-        compiler_params=pltpu.CompilerParams(vmem_limit_bytes=66800000, collective_id=0, has_side_effects=True),
+        compiler_params=pltpu.CompilerParams(vmem_limit_bytes=40 << 20, collective_id=0, has_side_effects=True),
         name="advect_solve_exchange",
-    )(tracers, offsets, weights, diffusion, send_index[0], send_count)
+    )(*(pltpu.with_memory_space_constraint(x, pltpu.HBM) for x in (tracers, offsets, weights, diffusion, send_index[0], send_count)))
     owned = pl.pallas_call(
         place_kernel,
         out_shape=jax.ShapeDtypeStruct((LEV, NTR, columns), jnp.float32),
         in_specs=[vmem, smem],
-        out_specs=vmem,
-        scratch_shapes=[pltpu.VMEM(((columns // LANES + 2) * FEAT, LANES), jnp.float32)],
+        out_specs=pl.BlockSpec(memory_space=pltpu.HBM),
+        scratch_shapes=[
+            pltpu.VMEM(((columns // LANES + 2) * FEAT, LANES), jnp.float32),
+            pltpu.VMEM((LEV, NTR, columns), jnp.float32),
+            pltpu.SemaphoreType.DMA((OUT_PIECES,)),
+        ],
         compiler_params=pltpu.CompilerParams(vmem_limit_bytes=32 << 20),
         name="place_owned",
     )(arrived, lengths)

time: 53.8 us -> 46.7 us (0.87)
  Pallas kernels: 51.5 us -> 46.6 us
  local copies, waits for them, and re-layouts: 2.16 us -> 0 us
    pallas_call x1, Pallas kernels: 46.9 us -> 43.7 us  [body(): pl.pallas_call(exchange_kernel, out_shape=(jax.ShapeDtypeStruct((PEERS, F...]
    unnamed x4 -> x0, local copies, waits for them, and re-layouts: 2.16 us -> none
    pallas_call x1, Pallas kernels: 4.59 us -> 2.93 us  [body(): pl.pallas_call(place_kernel, out_shape=jax.ShapeDtypeStruct((LEV, NTR, co...]
where the time goes in v4:
time: 46.7 us; the launch traced here: 46.6 us
  Pallas kernels  46.6 us (100%)
    pallas_call x1, Pallas kernels, body(): pl.pallas_call(exchange_kernel, out_shape=(jax.ShapeDtypeStruct((PEERS, F...  43.7 us
    pallas_call x1, Pallas kernels, body(): pl.pallas_call(place_kernel, out_shape=jax.ShapeDtypeStruct((LEV, NTR, co...  2.93 us

profile of v4, /device:TPU:1, one launch (start us, length us, event | category | flops | bytes accessed | tf_op | source)
XLA Modules:
  0.0 46.6 jit_solution(12431062234529859609)
XLA Ops:
  0.0 43.7 %advect_solve_exchange.1 = (f32[128,32,128]{2,1,0:T(8,128)S(1)}, s32[1,128]{1,0:T(1,128)S(1)}) custom-call(f32[3,10,64,128]{3,2,1,0:T(8,128)} %tracers_hbm.1, s32[10,64,128]{2,1,0:T(8,128)} %offsets_hbm.1, f32[10,64,128]{2,1,0:T(8,128)} %weights_hbm.1, f32[9,64,128]{2,1,0:T(8,128)} %diffusion_hbm.1, s32[128,128]{1,0:T(8,128)} %bitcast.2, s32[1,128]{1,0:T(1,128)} %count_hbm.1), custom_call_target="tpu_custom_call" | custom-call | tf_op jit(solution)/shard_map/advect_solve_exchange/pallas_call | solution.py:320
  43.7 2.9 %place_owned.1 = f32[10,3,8192]{2,1,0:T(4,128)} custom-call(f32[128,32,128]{2,1,0:T(8,128)S(1)} %get-tuple-element.7.arrived, s32[1,128]{1,0:T(1,128)S(1)} %get-tuple-element.8.lengths), custom_call_target="tpu_custom_call" | custom-call | tf_op jit(solution)/shard_map/place_owned/pallas_call | solution.py:354

commit v5 on v4

--- a/solution.py
+++ b/solution.py
@@ -14,20 +14,10 @@
 FOUR = LANES // FEAT
 EDGES = LANES // HALO
 PEERS = 128
-ROW = 16
 PIECE = 2
 OUT_PIECES = 4
 AXES = ("lon", "lat")
 MESH = pl.DeviceIdType.MESH
-
-
-def torus_target(lon, lat, shift, flip):
-    x, y, z, core = (lon // 8) % 4, lat * 2 + lon // 32, (lon // 2) % 4, lon % 2
-    x = (x + shift) % 4
-    y = (y + shift // 4 + shift) % 4
-    z = (z + shift // 16 + shift // 4 + shift) % 4
-    core = (core + flip) % 2
-    return (y % 2) * 32 + x * 8 + z * 2 + core, y // 2
 
 
 def factor_levels(coefs):
@@ -71,8 +61,7 @@
         (weights_hbm, weights), (diffusion_hbm, diffusion), (count_hbm, count),
     )
     loads = [pltpu.make_async_copy(source, here, load_sems.at[i]) for i, (source, here) in enumerate(pairs)]
-    for load in loads:
-        load.start()
+    loads[0].start()
     lat_rows = tracers.shape[2]
     groups = lat_rows // 8
     packs = from_east.shape[1]
@@ -80,21 +69,23 @@
     bands = lax.axis_size("lon")
     me = lon * 2 + lat
     lane = lax.broadcasted_iota(jnp.int32, (8, LANES), 1)
-    lane_group = lax.broadcasted_iota(jnp.int32, (LANES, LANES), 1) // FEAT
+    sublanes = lax.broadcasted_iota(jnp.int32, (8, LANES), 0)
 
     barrier = pltpu.get_barrier_semaphore()
 
-    row_first, in_row = (me // ROW) * ROW, lax.rem(me, ROW)
+    def digit_mates(low, span):
+        mask = span - low
+        return [(me & (PEERS - 1 - mask)) + ((me + low * step) & mask) for step in range(1, span // low)]
 
     def greet(semaphore, other):
-        pl.semaphore_signal(semaphore, inc=1, device_id=(other // 2, lax.rem(other, 2)), device_id_type=MESH)
-
-    for ring in (2, PEERS - 2):
-        greet(barrier, lax.rem(me + ring, PEERS))
-    for step in range(1, ROW):
-        greet(barrier, row_first + lax.rem(in_row + step, ROW))
-    for step in range(ROW, PEERS, ROW):
-        greet(barrier, lax.rem(me + step, PEERS))
+        pl.semaphore_signal(semaphore, inc=1, device_id=(other >> 1, other & 1), device_id_type=MESH)
+
+    ring = [(me + 2) & (PEERS - 1), (me - 2) & (PEERS - 1)]
+    entrance = ring + digit_mates(1, 4) + digit_mates(4, 16) + digit_mates(16, PEERS)
+    for other in entrance:
+        greet(barrier, other)
+    for load in loads[1:]:
+        load.start()
 
     loads[0].wait()
 
@@ -131,19 +122,19 @@
     for piece in range(pieces):
         lax.fori_loop(piece * PIECE, piece * PIECE + PIECE, pack_edges, 0, unroll=True)
         if piece == 0:
-            pl.semaphore_wait(barrier, 2 + ROW - 1 + PEERS // ROW - 1)
+            pl.semaphore_wait(barrier, len(entrance))
         for copy in edge_copies(piece):
             copy.start()
-    for step in range(1, ROW):
-        greet(ready, row_first + lax.rem(in_row + step, ROW))
+    for other in digit_mates(1, 4):
+        greet(ready.at[0], other)
 
     loads[1].wait()
     column = index[...]
     owner = lax.broadcasted_iota(jnp.int32, column.shape, 0)
-    member_of = ((owner // 16) % 4 - (lon // 8) % 4 + 4) % 4
-    row = column // LANES
-    turn_by = (member_of - row % 4 + 4) % 4
-    place[...] = turn_by * (lat_rows * LANES // 4) + (row // 4) * LANES + column % LANES
+    member_of = (owner // 16 - lon // 8) & 3
+    row = column >> 7
+    turn_by = (member_of - row) & 3
+    place[...] = turn_by * (lat_rows * LANES // 4) + (row >> 2) * LANES + (column & (LANES - 1))
     to_scalars = pltpu.make_async_copy(place, address, address_sem)
     to_scalars.start()
 
@@ -172,6 +163,9 @@
         return carry
 
     lax.fori_loop(0, groups, interior, 0)
+    pl.semaphore_wait(ready.at[0], 3)
+    for other in digit_mates(4, 16):
+        greet(ready.at[1], other)
 
     def finish(group, carry):
         at = pl.ds(pl.multiple_of(group * 8, 8), 8)
@@ -221,31 +215,42 @@
 
     table_rows = table.reshape(FOUR * lat_rows * LANES // FOUR, LANES)
 
+    x, y, z, core = (lon >> 3) & 3, lat * 2 + (lon >> 5), (lon >> 1) & 3, lon & 1
+
     def targets_of(step):
+        away = step & 15
+        to_core = (core + (step >> 4)) & 1
         targets = []
         for member in range(FOUR):
-            to_lon, to_lat = torus_target(lon, lat, (step // 2) * FOUR + member, step % 2)
+            to_x = (x + member) & 3
+            to_y = (y + (away & 3) + member) & 3
+            to_z = (z + ((away >> 2) + away) + member) & 3
+            to_lon = ((to_y & 1) << 5) + (to_x << 3) + (to_z << 1) + to_core
+            to_lat = to_y >> 1
             targets.append((to_lon, to_lat, to_lon * 2 + to_lat))
         return targets
 
     def gather(step, half):
         owners = [owner for _, _, owner in targets_of(step)]
-        for slot in range(LANES):
+        for eight in range(LANES // 8):
+            wide = None
             for member in range(FOUR):
-                at = address[owners[member], slot]
-                stage[half, member, slot : slot + 1, :] = table_rows[pl.ds(at, 1), :]
+                tile = None
+                for sublane in range(8):
+                    at = address[owners[member], eight * 8 + sublane]
+                    row = jnp.broadcast_to(table_rows[pl.ds(at, 1), :], (8, LANES))
+                    tile = row if tile is None else jnp.where(sublanes == sublane, row, tile)
+                wide = tile if wide is None else jnp.where(lane // FEAT == member, tile, wide)
+            stage[half, eight * 8 : eight * 8 + 8, :] = wide
 
     def send(step, half, first=0):
-        wide = stage[half, 0]
-        for member in range(1, FOUR):
-            wide = jnp.where(lane_group == member, stage[half, member], wide)
-        turned = wide.T
+        turned = stage[half].T
         for member, (to_lon, to_lat, owner) in enumerate(targets_of(step)):
             box = step * FOUR + member
             outbox[box] = turned[member * FEAT : (member + 1) * FEAT, :]
             length = count[0, owner].astype(jnp.float32)
             outbox[box, SENT - 1 : SENT, :] = jnp.full((1, LANES), length, jnp.float32)
-            slot = lax.rem(owner - me + PEERS, PEERS)
+            slot = (owner - me) & (PEERS - 1)
             if member >= first:
                 pltpu.make_async_remote_copy(
                     src_ref=outbox.at[box, 0:SENT], dst_ref=arrived.at[slot, 0:SENT],
@@ -254,7 +259,7 @@
                 ).start()
 
     to_scalars.wait()
-    pl.semaphore_wait(ready, ROW - 1)
+    pl.semaphore_wait(ready.at[1], 3)
     steps = PEERS // FOUR
     gather(0, 0)
     send(0, 0, first=1)
@@ -337,7 +342,7 @@
             edge, edge, edge, edge,
             pltpu.VMEM((lat_rows * FEAT, LANES), jnp.float32),
             pltpu.VMEM((FOUR, columns // FOUR, LANES), jnp.float32),
-            pltpu.VMEM((2, FOUR, LANES, LANES), jnp.float32),
+            pltpu.VMEM((2, LANES, LANES), jnp.float32),
             pltpu.VMEM((PEERS, FEAT, LANES), jnp.float32),
             pltpu.VMEM((PEERS, LANES), jnp.int32),
             pltpu.SMEM((PEERS, LANES), jnp.int32),
@@ -346,7 +351,7 @@
             pltpu.SemaphoreType.DMA,
             pltpu.SemaphoreType.DMA,
             pltpu.SemaphoreType.DMA,
-            pltpu.SemaphoreType.REGULAR,
+            pltpu.SemaphoreType.REGULAR((2,)),
         ],
         compiler_params=pltpu.CompilerParams(vmem_limit_bytes=40 << 20, collective_id=0, has_side_effects=True),
         name="advect_solve_exchange",

time: 46.7 us -> 45.3 us (0.970)
  Pallas kernels: 46.6 us -> 45.1 us
    pallas_call x1, Pallas kernels: 43.7 us -> 42.2 us  [body(): pl.pallas_call(exchange_kernel, out_shape=(jax.ShapeDtypeStruct((PEERS, F...]
where the time goes in v5:
time: 45.3 us; the launch traced here: 45.1 us
  Pallas kernels  45.1 us (100%)
    pallas_call x1, Pallas kernels, body(): pl.pallas_call(exchange_kernel, out_shape=(jax.ShapeDtypeStruct((PEERS, F...  42.2 us
    pallas_call x1, Pallas kernels, body(): pl.pallas_call(place_kernel, out_shape=jax.ShapeDtypeStruct((LEV, NTR, co...  2.93 us

profile of v5, /device:TPU:1, one launch (start us, length us, event | category | flops | bytes accessed | tf_op | source)
XLA Modules:
  0.0 45.1 jit_solution(17093239067454232438)
XLA Ops:
  0.0 42.2 %advect_solve_exchange.1 = (f32[128,32,128]{2,1,0:T(8,128)S(1)}, s32[1,128]{1,0:T(1,128)S(1)}) custom-call(f32[3,10,64,128]{3,2,1,0:T(8,128)} %tracers_hbm.1, s32[10,64,128]{2,1,0:T(8,128)} %offsets_hbm.1, f32[10,64,128]{2,1,0:T(8,128)} %weights_hbm.1, f32[9,64,128]{2,1,0:T(8,128)} %diffusion_hbm.1, s32[128,128]{1,0:T(8,128)} %bitcast.2, s32[1,128]{1,0:T(1,128)} %count_hbm.1), custom_call_target="tpu_custom_call" | custom-call | tf_op jit(solution)/shard_map/advect_solve_exchange/pallas_call | solution.py:325
  42.2 2.9 %place_owned.1 = f32[10,3,8192]{2,1,0:T(4,128)} custom-call(f32[128,32,128]{2,1,0:T(8,128)S(1)} %get-tuple-element.7.arrived, s32[1,128]{1,0:T(1,128)S(1)} %get-tuple-element.8.lengths), custom_call_target="tpu_custom_call" | custom-call | tf_op jit(solution)/shard_map/place_owned/pallas_call | solution.py:359

commit v6 on v5

--- a/solution.py
+++ b/solution.py
@@ -9,7 +9,8 @@
 LEV = 10
 HALO = 16
 FEAT = 32
-SENT = NTR * LEV + 1
+SENT = NTR * LEV
+FAR_OUT = 1000.0
 LANES = 128
 FOUR = LANES // FEAT
 EDGES = LANES // HALO
@@ -243,42 +244,44 @@
                 wide = tile if wide is None else jnp.where(lane // FEAT == member, tile, wide)
             stage[half, eight * 8 : eight * 8 + 8, :] = wide
 
-    def send(step, half, first=0):
+    def send(step, half):
         turned = stage[half].T
         for member, (to_lon, to_lat, owner) in enumerate(targets_of(step)):
             box = step * FOUR + member
             outbox[box] = turned[member * FEAT : (member + 1) * FEAT, :]
-            length = count[0, owner].astype(jnp.float32)
-            outbox[box, SENT - 1 : SENT, :] = jnp.full((1, LANES), length, jnp.float32)
+            length = jnp.full((1, LANES), count[0, owner].astype(jnp.float32), jnp.float32)
+            unused = (lane[0:1] == LANES - 1) & (length < LANES)
+            outbox[box, 0:1, :] = jnp.where(unused, length + FAR_OUT, turned[member * FEAT : member * FEAT + 1, :])
             slot = (owner - me) & (PEERS - 1)
-            if member >= first:
+
+            def start():
                 pltpu.make_async_remote_copy(
                     src_ref=outbox.at[box, 0:SENT], dst_ref=arrived.at[slot, 0:SENT],
                     send_sem=send_sem, recv_sem=recv_sem,
                     device_id=(to_lon, to_lat), device_id_type=MESH,
                 ).start()
 
+            if member or half:
+                start()
+            else:
+                pl.when(step > 0)(start)
+
     to_scalars.wait()
     pl.semaphore_wait(ready.at[1], 3)
     steps = PEERS // FOUR
-    gather(0, 0)
-    send(0, 0, first=1)
-    gather(1, 1)
-
     def two_steps(turn_at, carry):
-        send(2 * turn_at + 1, 1)
-        gather(2 * turn_at + 2, 0)
-        send(2 * turn_at + 2, 0)
-        gather(2 * turn_at + 3, 1)
-        return carry
-
-    lax.fori_loop(0, steps // 2 - 1, two_steps, 0)
-    send(steps - 1, 1)
+        for half in range(2):
+            gather(2 * turn_at + half, half)
+            send(2 * turn_at + half, half)
+        return carry
+
+    lax.fori_loop(0, steps // 2, two_steps, 0)
     arrived[0] = outbox[0]
     others = pltpu.make_async_copy(outbox.at[1:PEERS, 0:SENT], arrived.at[1:PEERS, 0:SENT], recv_sem)
     others.wait()
     pltpu.make_async_copy(outbox.at[1:PEERS, 0:SENT], arrived.at[1:PEERS, 0:SENT], send_sem).wait()
-    lengths[...] = arrived[:, SENT - 1, :].T[0:1, :].astype(jnp.int32)
+    last = arrived[:, 0, :].T[LANES - 1 : LANES, :]
+    lengths[...] = jnp.where(last > FAR_OUT / 2, last - FAR_OUT, LANES).astype(jnp.int32)
     for piece in range(pieces):
         for copy in edge_copies(piece):
             copy.wait_send()

time: 45.3 us -> 44.4 us (0.980)
  Pallas kernels: 45.1 us -> 44.2 us
    pallas_call x1, Pallas kernels: 42.2 us -> 41.3 us  [body(): pl.pallas_call(exchange_kernel, out_shape=(jax.ShapeDtypeStruct((PEERS, F...]
where the time goes in v6:
time: 44.4 us; the launch traced here: 44.2 us
  Pallas kernels  44.2 us (100%)
    pallas_call x1, Pallas kernels, body(): pl.pallas_call(exchange_kernel, out_shape=(jax.ShapeDtypeStruct((PEERS, F...  41.3 us
    pallas_call x1, Pallas kernels, body(): pl.pallas_call(place_kernel, out_shape=jax.ShapeDtypeStruct((LEV, NTR, co...  2.93 us

profile of v6, /device:TPU:1, one launch (start us, length us, event | category | flops | bytes accessed | tf_op | source)
XLA Modules:
  0.0 44.2 jit_solution(15432899382672720048)
XLA Ops:
  0.0 41.3 %advect_solve_exchange.1 = (f32[128,32,128]{2,1,0:T(8,128)S(1)}, s32[1,128]{1,0:T(1,128)S(1)}) custom-call(f32[3,10,64,128]{3,2,1,0:T(8,128)} %tracers_hbm.1, s32[10,64,128]{2,1,0:T(8,128)} %offsets_hbm.1, f32[10,64,128]{2,1,0:T(8,128)} %weights_hbm.1, f32[9,64,128]{2,1,0:T(8,128)} %diffusion_hbm.1, s32[128,128]{1,0:T(8,128)} %bitcast.2, s32[1,128]{1,0:T(1,128)} %count_hbm.1), custom_call_target="tpu_custom_call" | custom-call | tf_op jit(solution)/shard_map/advect_solve_exchange/pallas_call | solution.py:328
  41.3 2.9 %place_owned.1 = f32[10,3,8192]{2,1,0:T(4,128)} custom-call(f32[128,32,128]{2,1,0:T(8,128)S(1)} %get-tuple-element.7.arrived, s32[1,128]{1,0:T(1,128)S(1)} %get-tuple-element.8.lengths), custom_call_target="tpu_custom_call" | custom-call | tf_op jit(solution)/shard_map/place_owned/pallas_call | solution.py:362

commit v7 on v6

--- a/solution.py
+++ b/solution.py
@@ -16,7 +16,7 @@
 EDGES = LANES // HALO
 PEERS = 128
 PIECE = 2
-OUT_PIECES = 4
+OUT_PIECES = 2
 AXES = ("lon", "lat")
 MESH = pl.DeviceIdType.MESH
 
@@ -163,13 +163,13 @@
             factors[LEV + level, at, :] = uppers[level]
         return carry
 
-    lax.fori_loop(0, groups, interior, 0)
+    lax.fori_loop(0, groups, interior, 0, unroll=8)
     pl.semaphore_wait(ready.at[0], 3)
     for other in digit_mates(4, 16):
         greet(ready.at[1], other)
 
-    def finish(group, carry):
-        at = pl.ds(pl.multiple_of(group * 8, 8), 8)
+    def finish(group):
+        at = pl.ds(group * 8, 8)
         values = [[None] * LEV for _ in range(NTR)]
         for level in range(LEV):
             cell = lane + offsets[level, at, :]
@@ -194,25 +194,24 @@
                 rows[pl.ds(group * 8 * FEAT + level * NTR + t, 8, stride=FEAT), :] = solved[level]
         for spare in range(NTR * LEV, FEAT):
             rows[pl.ds(group * 8 * FEAT + spare, 8, stride=FEAT), :] = jnp.zeros((8, LANES), jnp.float32)
-        return carry
-
-    def turn(block, carry):
-        at = pl.ds(pl.multiple_of(block * LANES, LANES), LANES)
+
+    def turn(block):
+        at = pl.ds(block * LANES, LANES)
         turned = rows[at, :].T
         for by in range(FOUR):
             table[by, at, :] = pltpu.roll(turned, by * FEAT, 1) if by else turned
-        return carry
-
-    def finish_piece(piece, carry):
-        for copy in edge_copies(piece):
-            copy.wait_recv()
-        lax.fori_loop(piece * PIECE, piece * PIECE + PIECE, finish, 0)
-        blocks = PIECE * 8 // FOUR
-        for block in range(blocks):
-            turn(piece * blocks + block, 0)
-        return carry
-
-    lax.fori_loop(0, pieces, finish_piece, 0)
+
+    blocks = PIECE * 8 // FOUR
+    for piece in range(pieces + 1):
+        if piece < pieces:
+            for copy in edge_copies(piece):
+                copy.wait_recv()
+        for part in range(PIECE):
+            if piece < pieces:
+                finish(piece * PIECE + part)
+            if piece:
+                for block in range(blocks // PIECE):
+                    turn((piece - 1) * blocks + part * (blocks // PIECE) + block)
 
     table_rows = table.reshape(FOUR * lat_rows * LANES // FOUR, LANES)
 
@@ -301,7 +300,7 @@
         owned[second, :] = rolled
         return start + lengths[0, source]
 
-    lax.fori_loop(0, arrived.shape[0], place, jnp.int32(0), unroll=16)
+    lax.fori_loop(0, arrived.shape[0], place, jnp.int32(0), unroll=32)
 
     copies = []
     width = columns // OUT_PIECES

time: 44.4 us -> 42.9 us (0.966)
  Pallas kernels: 44.2 us -> 42.5 us
    pallas_call x1, Pallas kernels: 41.3 us -> 39.8 us  [body(): pl.pallas_call(exchange_kernel, out_shape=(jax.ShapeDtypeStruct((PEERS, F...]
where the time goes in v7:
time: 42.9 us; the launch traced here: 42.5 us
  Pallas kernels  42.5 us (99%)
    pallas_call x1, Pallas kernels, body(): pl.pallas_call(exchange_kernel, out_shape=(jax.ShapeDtypeStruct((PEERS, F...  39.8 us
    pallas_call x1, Pallas kernels, body(): pl.pallas_call(place_kernel, out_shape=jax.ShapeDtypeStruct((LEV, NTR, co...  2.77 us

profile of v7, /device:TPU:1, one launch (start us, length us, event | category | flops | bytes accessed | tf_op | source)
XLA Modules:
  0.0 42.5 jit_solution(14261712648702569144)
XLA Ops:
  0.0 39.8 %advect_solve_exchange.1 = (f32[128,32,128]{2,1,0:T(8,128)S(1)}, s32[1,128]{1,0:T(1,128)S(1)}) custom-call(f32[3,10,64,128]{3,2,1,0:T(8,128)} %tracers_hbm.1, s32[10,64,128]{2,1,0:T(8,128)} %offsets_hbm.1, f32[10,64,128]{2,1,0:T(8,128)} %weights_hbm.1, f32[9,64,128]{2,1,0:T(8,128)} %diffusion_hbm.1, s32[128,128]{1,0:T(8,128)} %bitcast.2, s32[1,128]{1,0:T(1,128)} %count_hbm.1), custom_call_target="tpu_custom_call" | custom-call | tf_op jit(solution)/shard_map/advect_solve_exchange/pallas_call | solution.py:327
  39.8 2.8 %place_owned.1 = f32[10,3,8192]{2,1,0:T(4,128)} custom-call(f32[128,32,128]{2,1,0:T(8,128)S(1)} %get-tuple-element.7.arrived, s32[1,128]{1,0:T(1,128)S(1)} %get-tuple-element.8.lengths), custom_call_target="tpu_custom_call" | custom-call | tf_op jit(solution)/shard_map/place_owned/pallas_call | solution.py:361

commit v8 on v7

--- a/solution.py
+++ b/solution.py
@@ -15,8 +15,8 @@
 FOUR = LANES // FEAT
 EDGES = LANES // HALO
 PEERS = 128
-PIECE = 2
-OUT_PIECES = 2
+PIECE = 4
+OUT_PIECES = 1
 AXES = ("lon", "lat")
 MESH = pl.DeviceIdType.MESH
 
@@ -55,14 +55,19 @@
     tracers_hbm, offsets_hbm, weights_hbm, diffusion_hbm, index_hbm, count_hbm, arrived, lengths,
     tracers, offsets, weights, diffusion, index, count, partial, factors,
     edge_low, edge_high, from_east, from_west, rows, table, stage, outbox, place, address,
-    load_sems, edge_sems, address_sem, send_sem, recv_sem, ready,
+    load_sems, edge_sems, address_sem, send_sem, recv_sem, ready, tracer_sems,
 ):
     pairs = (
-        (tracers_hbm, tracers), (index_hbm, index), (offsets_hbm, offsets),
+        (index_hbm, index), (offsets_hbm, offsets),
         (weights_hbm, weights), (diffusion_hbm, diffusion), (count_hbm, count),
     )
     loads = [pltpu.make_async_copy(source, here, load_sems.at[i]) for i, (source, here) in enumerate(pairs)]
-    loads[0].start()
+    def tracer_load(piece):
+        at = pl.ds(piece * PIECE * 8, PIECE * 8)
+        return pltpu.make_async_copy(tracers_hbm.at[:, :, at], tracers.at[:, :, at], tracer_sems.at[piece])
+
+    for piece in range(tracers.shape[2] // (PIECE * 8)):
+        tracer_load(piece).start()
     lat_rows = tracers.shape[2]
     groups = lat_rows // 8
     packs = from_east.shape[1]
@@ -85,10 +90,8 @@
     entrance = ring + digit_mates(1, 4) + digit_mates(4, 16) + digit_mates(16, PEERS)
     for other in entrance:
         greet(barrier, other)
-    for load in loads[1:]:
+    for load in loads:
         load.start()
-
-    loads[0].wait()
 
     def pack_edges(group, carry):
         at = pl.ds(pl.multiple_of(group * 8, 8), 8)
@@ -121,6 +124,7 @@
 
     pieces = groups // PIECE
     for piece in range(pieces):
+        tracer_load(piece).wait()
         lax.fori_loop(piece * PIECE, piece * PIECE + PIECE, pack_edges, 0, unroll=True)
         if piece == 0:
             pl.semaphore_wait(barrier, len(entrance))
@@ -129,7 +133,7 @@
     for other in digit_mates(1, 4):
         greet(ready.at[0], other)
 
-    loads[1].wait()
+    loads[0].wait()
     column = index[...]
     owner = lax.broadcasted_iota(jnp.int32, column.shape, 0)
     member_of = (owner // 16 - lon // 8) & 3
@@ -139,7 +143,7 @@
     to_scalars = pltpu.make_async_copy(place, address, address_sem)
     to_scalars.start()
 
-    for load in loads[2:]:
+    for load in loads[1:]:
         load.wait()
 
     def interior(group, carry):
@@ -300,7 +304,7 @@
         owned[second, :] = rolled
         return start + lengths[0, source]
 
-    lax.fori_loop(0, arrived.shape[0], place, jnp.int32(0), unroll=32)
+    lax.fori_loop(0, arrived.shape[0], place, jnp.int32(0), unroll=128)
 
     copies = []
     width = columns // OUT_PIECES
@@ -348,12 +352,13 @@
             pltpu.VMEM((PEERS, FEAT, LANES), jnp.float32),
             pltpu.VMEM((PEERS, LANES), jnp.int32),
             pltpu.SMEM((PEERS, LANES), jnp.int32),
-            pltpu.SemaphoreType.DMA((6,)),
+            pltpu.SemaphoreType.DMA((5,)),
             pltpu.SemaphoreType.DMA((2, 2, groups // PIECE)),
             pltpu.SemaphoreType.DMA,
             pltpu.SemaphoreType.DMA,
             pltpu.SemaphoreType.DMA,
             pltpu.SemaphoreType.REGULAR((2,)),
+            pltpu.SemaphoreType.DMA((groups // PIECE,)),
         ],
         compiler_params=pltpu.CompilerParams(vmem_limit_bytes=40 << 20, collective_id=0, has_side_effects=True),
         name="advect_solve_exchange",

time: 42.9 us -> 42.9 us (level)
  no operation moved by 1% of the time
where the time goes in v8:
time: 42.9 us; the launch traced here: 42.8 us
  Pallas kernels  42.7 us (100%)
    pallas_call x1, Pallas kernels, body(): pl.pallas_call(exchange_kernel, out_shape=(jax.ShapeDtypeStruct((PEERS, F...  40 us
    pallas_call x1, Pallas kernels, body(): pl.pallas_call(place_kernel, out_shape=jax.ShapeDtypeStruct((LEV, NTR, co...  2.72 us

profile of v8, /device:TPU:1, one launch (start us, length us, event | category | flops | bytes accessed | tf_op | source)
XLA Modules:
  0.0 42.8 jit_solution(5481457034003097286)
XLA Ops:
  0.0 40.0 %advect_solve_exchange.1 = (f32[128,32,128]{2,1,0:T(8,128)S(1)}, s32[1,128]{1,0:T(1,128)S(1)}) custom-call(f32[3,10,64,128]{3,2,1,0:T(8,128)} %tracers_hbm.1, s32[10,64,128]{2,1,0:T(8,128)} %offsets_hbm.1, f32[10,64,128]{2,1,0:T(8,128)} %weights_hbm.1, f32[9,64,128]{2,1,0:T(8,128)} %diffusion_hbm.1, s32[128,128]{1,0:T(8,128)} %bitcast.2, s32[1,128]{1,0:T(1,128)} %count_hbm.1), custom_call_target="tpu_custom_call" | custom-call | tf_op jit(solution)/shard_map/advect_solve_exchange/pallas_call | solution.py:331
  40.0 2.7 %place_owned.1 = f32[10,3,8192]{2,1,0:T(4,128)} custom-call(f32[128,32,128]{2,1,0:T(8,128)S(1)} %get-tuple-element.7.arrived, s32[1,128]{1,0:T(1,128)S(1)} %get-tuple-element.8.lengths), custom_call_target="tpu_custom_call" | custom-call | tf_op jit(solution)/shard_map/place_owned/pallas_call | solution.py:366

commit v9 on v8

--- a/solution.py
+++ b/solution.py
@@ -242,7 +242,7 @@
                 tile = None
                 for sublane in range(8):
                     at = address[owners[member], eight * 8 + sublane]
-                    row = jnp.broadcast_to(table_rows[pl.ds(at, 1), :], (8, LANES))
+                    row = table_rows[pl.ds(at, 8, stride=0), :]
                     tile = row if tile is None else jnp.where(sublanes == sublane, row, tile)
                 wide = tile if wide is None else jnp.where(lane // FEAT == member, tile, wide)
             stage[half, eight * 8 : eight * 8 + 8, :] = wide
@@ -295,8 +295,8 @@
     lane = lax.broadcasted_iota(jnp.int32, (FEAT, LANES), 1)
 
     def place(source, start):
-        block = start // LANES
-        shift = lax.rem(start, LANES)
+        block = start >> 7
+        shift = start & (LANES - 1)
         rolled = pltpu.roll(arrived[source], shift, 1)
         first = pl.ds(pl.multiple_of(block * FEAT, FEAT), FEAT)
         second = pl.ds(pl.multiple_of(block * FEAT + FEAT, FEAT), FEAT)

time: 42.9 us -> 42.6 us (level)
  no operation moved by 1% of the time
where the time goes in v9:
time: 42.6 us; the launch traced here: 42.5 us
  Pallas kernels  42.5 us (100%)
    pallas_call x1, Pallas kernels, body(): pl.pallas_call(exchange_kernel, out_shape=(jax.ShapeDtypeStruct((PEERS, F...  40 us
    pallas_call x1, Pallas kernels, body(): pl.pallas_call(place_kernel, out_shape=jax.ShapeDtypeStruct((LEV, NTR, co...  2.49 us

profile of v9, /device:TPU:1, one launch (start us, length us, event | category | flops | bytes accessed | tf_op | source)
XLA Modules:
  0.0 42.5 jit_solution(97686631561569524)
XLA Ops:
  0.0 40.0 %advect_solve_exchange.1 = (f32[128,32,128]{2,1,0:T(8,128)S(1)}, s32[1,128]{1,0:T(1,128)S(1)}) custom-call(f32[3,10,64,128]{3,2,1,0:T(8,128)} %tracers_hbm.1, s32[10,64,128]{2,1,0:T(8,128)} %offsets_hbm.1, f32[10,64,128]{2,1,0:T(8,128)} %weights_hbm.1, f32[9,64,128]{2,1,0:T(8,128)} %diffusion_hbm.1, s32[128,128]{1,0:T(8,128)} %bitcast.2, s32[1,128]{1,0:T(1,128)} %count_hbm.1), custom_call_target="tpu_custom_call" | custom-call | tf_op jit(solution)/shard_map/advect_solve_exchange/pallas_call | solution.py:331
  40.0 2.5 %place_owned.1 = f32[10,3,8192]{2,1,0:T(4,128)} custom-call(f32[128,32,128]{2,1,0:T(8,128)S(1)} %get-tuple-element.7.arrived, s32[1,128]{1,0:T(1,128)S(1)} %get-tuple-element.8.lengths), custom_call_target="tpu_custom_call" | custom-call | tf_op jit(solution)/shard_map/place_owned/pallas_call | solution.py:366
